TPU v7x, 32 devices: a whole 2x2x4 slice. The times are simulated.
32 devices in a mesh: dp: 2 (over x), expert: 16 (over z, y, core).
Axes of the slice: x: 2, y: 2, z: 4, core: 2. Of those that a mesh axis runs over, the one named last changes fastest.
Arguments:
- tokens: bfloat16 [4096, 7168], P('expert', 'dp'), may hold values from -6 to 6
- cotangent: bfloat16 [4096, 7168], P('expert', 'dp'), may hold values from -6 to 6
- routing: int32 [4096, 8], P('expert'), may hold values from 0 to 255, as said below
- gate_values: float32 [4096, 8], P('expert'), may hold values from 0.05 to 0.6
- hidden_weight: bfloat16 [16, 7168, 2048], P('expert', 'dp'), may hold values from -0.0625 to 0.0625
- output_weight: bfloat16 [16, 1024, 7168], P('expert', None, 'dp'), may hold values from -0.1875 to 0.1875
Outputs:
- mixed: bfloat16 [4096, 7168], P('expert', 'dp')
- token_grad: bfloat16 [4096, 7168], P('expert', 'dp')
- hidden_grad: bfloat16 [16, 7168, 2048], P('expert', 'dp')
- output_grad: bfloat16 [16, 1024, 7168], P('expert', None, 'dp')
Inputs may be any that keep to these rules, and one draw needn't show every extreme that they name: `routing`: each row names 8 different experts. Within the 256 rows of one index of expert no expert is named by more than 16 rows, and in every such block some experts below 16 are named by exactly 16 rows.
All inputs are finite; a program needn't handle non-finite values.
Results may differ from a plain program's by a relative error of at most 0.022.
Values may be sent and summed in bfloat16 or wider, within the bound.
No kernel may reach another device: no remote copies, remote signals or barrier semaphores. Data moves between devices by JAX's collectives and lax.ppermute only.
A program may use at most 128 MiB of HBM per device.

v0:
```python
import jax
import jax.numpy as jnp
from jax import lax
from jax.sharding import PartitionSpec as P

ROUTED = 256


def slot_table(routing_block, gate_block, expert_count, slot_count):
    tok_count = routing_block.shape[0]
    picked = routing_block.reshape(-1)
    onehot = (picked[:, None] == jnp.arange(expert_count, dtype=jnp.int32)[None, :]).astype(
        jnp.int32
    )
    earlier = jnp.cumsum(onehot, axis=0) - onehot
    ranking = jnp.sum(earlier * onehot, axis=1)
    slot_index = (picked * slot_count + ranking).reshape(tok_count, -1)
    target = jnp.arange(expert_count * slot_count, dtype=jnp.int32)
    matched = slot_index[None, :, :] == target[:, None, None]
    placed = jnp.any(matched, axis=2).astype(jnp.float32)
    gate_slot = jnp.sum(
        jnp.where(matched, gate_block[None, :, :], jnp.zeros_like(gate_block)[None, :, :]),
        axis=(1, 2),
    )
    return (placed, gate_slot)


def activate(hidden, half_width):
    gate_part = hidden[:, :half_width]
    up_part = hidden[:, half_width:]
    return (gate_part * jax.nn.sigmoid(gate_part) * up_part).astype(jnp.bfloat16)


def activate_grad(hidden, act_grad, half_width):
    gate_part = hidden[:, :half_width]
    up_part = hidden[:, half_width:]
    sigmoid_gate = jax.nn.sigmoid(gate_part)
    gate_grad = act_grad * up_part * sigmoid_gate * (1.0 + gate_part * (1.0 - sigmoid_gate))
    up_grad = act_grad * gate_part * sigmoid_gate
    return jnp.concatenate([gate_grad, up_grad], axis=1).astype(jnp.bfloat16)


def body(tokens, cotangent, routing, gate_values, hidden_weight, output_weight):
    tok_count, column_width = tokens.shape
    pick_count = routing.shape[1]
    expert_count = lax.axis_size("expert")
    slot_count = 2 * tok_count * pick_count // ROUTED
    row_total = expert_count * slot_count
    contract_cols = (((1,), (1,)), ((), ()))
    contract_rows = (((0,), (0,)), ((), ()))
    placed, gate_slot = slot_table(routing, gate_values, expert_count, slot_count)
    placed_half = placed.astype(jnp.bfloat16)
    send_shape = (expert_count, slot_count, column_width)
    token_rows = (
        jnp.dot(placed_half, tokens, preferred_element_type=jnp.float32)
        .astype(jnp.bfloat16)
        .reshape(send_shape)
    )
    cot_rows = (
        (gate_slot[:, None] * jnp.dot(placed_half, cotangent, preferred_element_type=jnp.float32))
        .astype(jnp.bfloat16)
        .reshape(send_shape)
    )
    inner_weight = hidden_weight[0]
    outer_weight = output_weight[0]
    half_width = outer_weight.shape[0]
    arrived = (
        lax.all_to_all(token_rows, "expert", split_axis=0, concat_axis=0, tiled=True),
        lax.all_to_all(cot_rows, "expert", split_axis=0, concat_axis=0, tiled=True),
    )
    expert_rows = arrived[0].reshape(row_total, column_width)
    scaled_cot = arrived[1].reshape(row_total, column_width)
    picked_rows = expert_rows
    hidden = lax.psum_scatter(
        jnp.dot(picked_rows, inner_weight, preferred_element_type=jnp.float32).astype(jnp.bfloat16),
        "dp",
        scatter_dimension=0,
        tiled=True,
    ).astype(jnp.float32)
    active = lax.all_gather(activate(hidden, half_width), "dp", axis=0, tiled=True)
    expert_out = jnp.dot(active, outer_weight, preferred_element_type=jnp.float32).astype(
        jnp.bfloat16
    )
    picked_rows = scaled_cot
    act_part = lax.psum_scatter(
        lax.dot_general(
            picked_rows, outer_weight, contract_cols, preferred_element_type=jnp.float32
        ).astype(jnp.bfloat16),
        "dp",
        scatter_dimension=0,
        tiled=True,
    ).astype(jnp.float32)
    hidden_cot = lax.all_gather(
        activate_grad(hidden, act_part, half_width), "dp", axis=0, tiled=True
    )
    output_grad = lax.dot_general(
        active, scaled_cot, contract_rows, preferred_element_type=jnp.float32
    ).astype(jnp.bfloat16)
    hidden_grad = lax.dot_general(
        expert_rows, hidden_cot, contract_rows, preferred_element_type=jnp.float32
    ).astype(jnp.bfloat16)
    row_grad = lax.dot_general(
        hidden_cot, inner_weight, contract_cols, preferred_element_type=jnp.float32
    ).astype(jnp.bfloat16)
    returned = (
        lax.all_to_all(
            expert_out.reshape(send_shape), "expert", split_axis=0, concat_axis=0, tiled=True
        ),
        lax.all_to_all(
            row_grad.reshape(send_shape), "expert", split_axis=0, concat_axis=0, tiled=True
        ),
    )
    back_out = returned[0]
    back_grad = returned[1]
    back_out = back_out.reshape(row_total, column_width)
    back_grad = back_grad.reshape(row_total, column_width)
    weighted = placed * gate_slot[:, None]
    mixed = lax.dot_general(
        weighted,
        back_out.astype(jnp.float32),
        contract_rows,
        precision=lax.Precision.HIGHEST,
        preferred_element_type=jnp.float32,
    ).astype(jnp.bfloat16)
    token_grad = lax.dot_general(
        placed_half, back_grad, contract_rows, preferred_element_type=jnp.float32
    ).astype(jnp.bfloat16)
    return (mixed, token_grad, hidden_grad[None], output_grad[None])


def solution(mesh):
    return jax.shard_map(
        body,
        mesh=mesh,
        in_specs=(
            P("expert", "dp"),
            P("expert", "dp"),
            P("expert", None),
            P("expert", None),
            P("expert", "dp", None),
            P("expert", None, "dp"),
        ),
        out_specs=(
            P("expert", "dp"),
            P("expert", "dp"),
            P("expert", "dp", None),
            P("expert", None, "dp"),
        ),
        check_vma=False,
    )
```

profile of v0, /device:TPU:13, one launch (start us, length us, event | category | flops | bytes accessed | tf_op | source)
XLA Modules:
  0.0 254.4 jit_solution(11101133766657065394)
XLA Ops:
  7.2 1.0 copy.22
  8.4 4.5 %reduce-window.6 = s32[16,16,128]{2,1,0:T(8,128)S(1)} reduce-window(s32[16,16,128]{2,1,0:T(8,128)S(1)} %fusion.35, s32[]{:T(128)} %constant.6.clone.1), window={size=1x1x128 pad=0_0x0_0x127_0}, to_apply=%region_0.0 | reduce-window | flops 4161536 | bytes 262148 | tf_op jit(solution)/shard_map/reduce-window
  12.9 0.4 slice_reduce_fusion
  13.4 0.2 reduce-window.9
  13.9 0.7 multiply_add_fusion
  14.6 0.9 fusion.20
  15.5 1.9 convolution_convert_fusion.4
  17.4 6.7 %all-to-all-start = ((bf16[16,16,3584]{2,1,0:T(8,128)(2,1)}), bf16[16,16,3584]{2,1,0:T(8,128)(2,1)S(1)}, u32[]{:S(2)}, u32[]{:S(2)}) async-start(bf16[16,16,3584]{2,1,0:T(8,128)(2,1)} %bitcast.62), calls=%async_computation | async-start | bytes 3670016 | tf_op jit(solution)/shard_map/all_to_all | solution.py:68
  24.0 1.0 select_reduce_fusion
  25.0 3.4 %fusion.16 = bf16[256,3584]{1,0:T(8,128)(2,1)} fusion(bf16[256,3584]{1,0:T(8,128)(2,1)} %param.7, f32[256]{0:T(256)S(1)} %select_reduce_fusion, pred[256,256]{1,0:T(8,128)(4,1)S(1)} %fusion.20), kind=kOutput, calls=%fused_computation.15 | convolution fusion | flops 471728128 | bytes 3736576 | tf_op jit(solution)/shard_map/dot_general | solution.py:60
  28.4 37.4 %all-to-all-done = bf16[16,16,3584]{2,1,0:T(8,128)(2,1)S(1)} async-done(((bf16[16,16,3584]{2,1,0:T(8,128)(2,1)}), bf16[16,16,3584]{2,1,0:T(8,128)(2,1)S(1)}, u32[]{:S(2)}, u32[]{:S(2)}) %all-to-all-start) | async-done | bytes 1835040 | tf_op jit(solution)/shard_map/all_to_all | solution.py:68
  65.8 4.8 %all-to-all-start.2 = ((bf16[16,16,3584]{2,1,0:T(8,128)(2,1)}), bf16[16,16,3584]{2,1,0:T(8,128)(2,1)}, u32[]{:S(2)}, u32[]{:S(2)}) async-start(bf16[16,16,3584]{2,1,0:T(8,128)(2,1)} %bitcast.63), calls=%async_computation.3 | async-start | bytes 3670016 | tf_op jit(solution)/shard_map/all_to_all | solution.py:69
  70.6 8.5 %fusion.17 = bf16[256,2048]{1,0:T(8,128)(2,1)} fusion(bf16[256,3584]{1,0:T(8,128)(2,1)S(1)} %bitcast.60, bf16[1,3584,2048]{2,1,0:T(8,128)(2,1)} %param.10), kind=kOutput, calls=%fused_computation.19 | convolution fusion | flops 3758620672 | bytes 17563648 | tf_op jit(solution)/shard_map/dot_general | solution.py:75
  79.2 33.3 %all-to-all-done.2 = bf16[16,16,3584]{2,1,0:T(8,128)(2,1)} async-done(((bf16[16,16,3584]{2,1,0:T(8,128)(2,1)}), bf16[16,16,3584]{2,1,0:T(8,128)(2,1)}, u32[]{:S(2)}, u32[]{:S(2)}) %all-to-all-start.2) | async-done | bytes 1835040 | tf_op jit(solution)/shard_map/all_to_all | solution.py:69
  112.5 6.5 %fusion.21 = bf16[256,1024]{1,0:T(8,128)(2,1)} fusion(bf16[256,3584]{1,0:T(8,128)(2,1)} %bitcast.8, bf16[1,1024,3584]{2,1,0:T(8,128)(2,1)} %param.11), kind=kOutput, calls=%fused_computation.23 | convolution fusion | flops 1879310336 | bytes 9699328 | tf_op jit(solution)/shard_map/dot_general | solution.py:86
  119.1 1.1 convert_element_type.60
  120.2 12.9 %reduce-scatter.5.cloned.1.call-done = bf16[128,1024]{1,0:T(8,128)(2,1)} async-done(((bf16[256,1024]{1,0:T(8,128)(2,1)}), bf16[128,1024]{1,0:T(8,128)(2,1)}) %reduce-scatter.5.cloned.1.call-update) | async-done | bytes 262160 | tf_op jit(solution)/shard_map/reduce_scatter | solution.py:85
  133.1 1.3 fusion.26
  134.3 7.7 %all_gather.6 = bf16[256,1024]{1,0:T(8,128)(2,1)S(1)} all-gather(bf16[128,1024]{1,0:T(8,128)(2,1)S(1)} %get-tuple-element.6), channel_id=1, replica_groups=mesh['dp'=2,'expert'=16] {'dp'}, dimensions={0}, use_global_device_ids=true | all-gather | bytes 786432 | tf_op jit(solution)/shard_map/all_gather | solution.py:80
  142.1 6.4 %fusion.10 = bf16[256,3584]{1,0:T(8,128)(2,1)} fusion(bf16[256,1024]{1,0:T(8,128)(2,1)S(1)} %all_gather.6, bf16[1,1024,3584]{2,1,0:T(8,128)(2,1)} %param.11), kind=kOutput, calls=%fused_computation.13 | convolution fusion | flops 1879965696 | bytes 9699328 | tf_op jit(solution)/shard_map/dot_general | solution.py:81
  148.4 7.3 %all-to-all-start.1 = ((bf16[16,16,3584]{2,1,0:T(8,128)(2,1)}), bf16[16,16,3584]{2,1,0:T(8,128)(2,1)}, u32[]{:S(2)}, u32[]{:S(2)}) async-start(bf16[16,16,3584]{2,1,0:T(8,128)(2,1)} %bitcast.64), calls=%async_computation.2 | async-start | bytes 3670016 | tf_op jit(solution)/shard_map/all_to_all | solution.py:106
  155.8 0.2 all-gather.2.cloned.1.call-start
  156.0 0.8 pad_maximum_fusion
  156.8 22.7 %all-gather.2.cloned.1.call-done = bf16[256,2048]{1,0:T(8,128)(2,1)} async-done(((bf16[128,2048]{1,0:T(8,128)(2,1)}), bf16[256,2048]{1,0:T(8,128)(2,1)}) %all-gather.2.cloned.1.call-update) | async-done | bytes 1048592 | tf_op jit(solution)/shard_map/all_gather | solution.py:93
  179.5 10.8 %fusion.13 = bf16[256,3584]{1,0:T(8,128)(2,1)} fusion(bf16[256,2048]{1,0:T(8,128)(2,1)} %all-gather.2.cloned.1.call-done, bf16[1,3584,2048]{2,1,0:T(8,128)(2,1)} %param.10), kind=kOutput, calls=%fused_computation.14 | convolution fusion | flops 3759013888 | bytes 17563648 | tf_op jit(solution)/shard_map/dot_general | solution.py:102
  190.3 7.4 %all-to-all-done.1 = bf16[16,16,3584]{2,1,0:T(8,128)(2,1)} async-done(((bf16[16,16,3584]{2,1,0:T(8,128)(2,1)}), bf16[16,16,3584]{2,1,0:T(8,128)(2,1)}, u32[]{:S(2)}, u32[]{:S(2)}) %all-to-all-start.1) | async-done | bytes 1835040 | tf_op jit(solution)/shard_map/all_to_all | solution.py:106
  197.7 4.8 %all-to-all-start.3 = ((bf16[16,16,3584]{2,1,0:T(8,128)(2,1)}), bf16[16,16,3584]{2,1,0:T(8,128)(2,1)}, u32[]{:S(2)}, u32[]{:S(2)}) async-start(bf16[16,16,3584]{2,1,0:T(8,128)(2,1)} %bitcast.65), calls=%async_computation.5 | async-start | bytes 3670016 | tf_op jit(solution)/shard_map/all_to_all | solution.py:109
  202.4 6.7 %fusion.9 = bf16[1,1024,3584]{2,1,0:T(8,128)(2,1)} fusion(bf16[256,1024]{1,0:T(8,128)(2,1)S(1)} %all_gather.6, bf16[256,3584]{1,0:T(8,128)(2,1)} %bitcast.8), kind=kOutput, calls=%fused_computation.11 | convolution fusion | flops 1882718208 | bytes 9699328 | tf_op jit(solution)/shard_map/dot_general | solution.py:96
  209.2 7.6 %fusion.4 = bf16[1,3584,2048]{2,1,0:T(8,128)(2,1)} fusion(bf16[256,3584]{1,0:T(8,128)(2,1)S(1)} %bitcast.61, bf16[256,2048]{1,0:T(8,128)(2,1)S(1)} %copy-done.2), kind=kOutput, calls=%fused_computation.5 | convolution fusion | flops 3765436416 | bytes 17563648 | tf_op jit(solution)/shard_map/dot_general | solution.py:99
  216.8 4.4 %convolution_convert_fusion.3 = bf16[256,3584]{1,0:T(8,128)(2,1)} fusion(bf16[256,3584]{1,0:T(8,128)(2,1)} %bitcast.6, pred[256,256]{1,0:T(8,128)(4,1)S(1)} %fusion.20, f32[256]{0:T(256)S(1)} %select_reduce_fusion), kind=kOutput, calls=%fused_computation.17 | convolution fusion | flops 2819555328 | bytes 3736576 | tf_op jit(solution)/shard_map/dot_general | solution.py:118
  221.2 23.1 %all-to-all-done.3 = bf16[16,16,3584]{2,1,0:T(8,128)(2,1)} async-done(((bf16[16,16,3584]{2,1,0:T(8,128)(2,1)}), bf16[16,16,3584]{2,1,0:T(8,128)(2,1)}, u32[]{:S(2)}, u32[]{:S(2)}) %all-to-all-start.3) | async-done | bytes 1835040 | tf_op jit(solution)/shard_map/all_to_all | solution.py:109
  244.3 3.5 %convolution_convert_fusion.2 = bf16[256,3584]{1,0:T(8,128)(2,1)} fusion(bf16[256,3584]{1,0:T(8,128)(2,1)} %bitcast.10, pred[256,256]{1,0:T(8,128)(4,1)S(1)} %fusion.20), kind=kOutput, calls=%fused_computation.16 | convolution fusion | flops 470810624 | bytes 3735552 | tf_op jit(solution)/shard_map/dot_general | solution.py:125
  (21 shorter events, 0.7 us)
Async XLA Ops:
  7.2 8.3 %copy-start = (bf16[256,3584]{1,0:T(8,128)(2,1)S(1)}, bf16[256,3584]{1,0:T(8,128)(2,1)}, u32[]{:S(2)}) copy-start(bf16[256,3584]{1,0:T(8,128)(2,1)} %param.6) | copy-start | bytes 5505028
  17.3 6.7 %copy-start.3 = (f32[256,8]{0,1:T(8,128)S(1)}, f32[256,8]{0,1:T(8,128)}, u32[]{:S(2)}) copy-start(f32[256,8]{0,1:T(8,128)} %param.9) | copy-start | bytes 24580
  17.4 48.5 %all-to-all-start = ((bf16[16,16,3584]{2,1,0:T(8,128)(2,1)}), bf16[16,16,3584]{2,1,0:T(8,128)(2,1)S(1)}, u32[]{:S(2)}, u32[]{:S(2)}) async-start(bf16[16,16,3584]{2,1,0:T(8,128)(2,1)} %bitcast.62), calls=%async_computation | async-start | bytes 3670016 | tf_op jit(solution)/shard_map/all_to_all | solution.py:68
  65.8 46.7 %all-to-all-start.2 = ((bf16[16,16,3584]{2,1,0:T(8,128)(2,1)}), bf16[16,16,3584]{2,1,0:T(8,128)(2,1)}, u32[]{:S(2)}, u32[]{:S(2)}) async-start(bf16[16,16,3584]{2,1,0:T(8,128)(2,1)} %bitcast.63), calls=%async_computation.3 | async-start | bytes 3670016 | tf_op jit(solution)/shard_map/all_to_all | solution.py:69
  70.6 48.5 %reduce-scatter.3.cloned.1.call-start = ((), (), s32[]{:S(2)}) async-start(), calls=%async_computation.6 | async-start | bytes 1572864 | tf_op jit(solution)/shard_map/reduce_scatter | solution.py:74
  79.2 53.9 %reduce-scatter.5.cloned.1.call-start = ((), (), s32[]{:S(2)}) async-start(), calls=%async_computation.7 | async-start | bytes 786432 | tf_op jit(solution)/shard_map/reduce_scatter | solution.py:85
  148.4 49.2 %all-to-all-start.1 = ((bf16[16,16,3584]{2,1,0:T(8,128)(2,1)}), bf16[16,16,3584]{2,1,0:T(8,128)(2,1)}, u32[]{:S(2)}, u32[]{:S(2)}) async-start(bf16[16,16,3584]{2,1,0:T(8,128)(2,1)} %bitcast.64), calls=%async_computation.2 | async-start | bytes 3670016 | tf_op jit(solution)/shard_map/all_to_all | solution.py:106
  155.8 23.8 %all-gather.2.cloned.1.call-start = ((), (), s32[]{:S(2)}) async-start(), calls=%async_computation.8 | async-start | bytes 1572864 | tf_op jit(solution)/shard_map/all_gather | solution.py:93
  197.7 46.7 %all-to-all-start.3 = ((bf16[16,16,3584]{2,1,0:T(8,128)(2,1)}), bf16[16,16,3584]{2,1,0:T(8,128)(2,1)}, u32[]{:S(2)}, u32[]{:S(2)}) async-start(bf16[16,16,3584]{2,1,0:T(8,128)(2,1)} %bitcast.65), calls=%async_computation.5 | async-start | bytes 3670016 | tf_op jit(solution)/shard_map/all_to_all | solution.py:109
  202.4 6.8 %copy-start.2 = (bf16[256,2048]{1,0:T(8,128)(2,1)S(1)}, bf16[256,2048]{1,0:T(8,128)(2,1)}, u32[]{:S(2)}) copy-start(bf16[256,2048]{1,0:T(8,128)(2,1)} %all-gather.2.cloned.1.call-done) | copy-start | bytes 3145732
  244.3 3.5 %copy-start.1 = (bf16[256,3584]{1,0:T(8,128)(2,1)S(1)}, bf16[256,3584]{1,0:T(8,128)(2,1)}, u32[]{:S(2)}) copy-start(bf16[256,3584]{1,0:T(8,128)(2,1)} %param.6) | copy-start | bytes 5505028
Sparse Core Ops, SparseCore 0:
  79.3 20.8 reduce-scatter.2
  119.2 13.8 reduce-scatter.4
  158.7 20.7 all-gather.1
where the time goes:
time: 255 us; the launch traced here: 254 us
  waiting for transfers between devices  137 us (54%)
  matrix products  59.7 us (23%)
  starting transfers between devices  23.8 us (9%)
  between operations  13.9 us (5%)
  other arithmetic  10.7 us (4%)
  blocking collectives  7.71 us (3%)
    all_to_all x1, waiting for transfers between devices, body(): lax.all_to_all(token_rows, 'expert', split_axis=0, concat_axis=0, tiled=T...  37.4 us
    all_to_all x1, waiting for transfers between devices, body(): lax.all_to_all(cot_rows, 'expert', split_axis=0, concat_axis=0, tiled=True)  33.3 us
    all_to_all x1, waiting for transfers between devices, body(): lax.all_to_all(row_grad.reshape(send_shape), 'expert', split_axis=0, conc...  23.1 us
    all_gather x1, waiting for transfers between devices, body(): lax.all_gather(activate_grad(hidden, act_part, half_width), 'dp', axis=0,...  22.7 us
    reduce_scatter x1, waiting for transfers between devices, body(): lax.psum_scatter(lax.dot_general(picked_rows, outer_weight, contract_cols...  12.9 us
    dot_general x1, matrix products, body(): lax.dot_general(hidden_cot, inner_weight, contract_cols, preferred_elemen...  10.8 us
    dot_general x1, matrix products, body(): jnp.dot(picked_rows, inner_weight, preferred_element_type=jnp.float32)  8.5 us
    all_gather x1, blocking collectives, body(): lax.all_gather(activate(hidden, half_width), 'dp', axis=0, tiled=True)  7.71 us
  transfers between devices with their start and end apart: 7, of which 6 were waited for; matrix products, arithmetic and copies ran while one was open for 20% of the time, Pallas kernels for 0%

commit v1 on v0

--- a/solution.py
+++ b/solution.py
@@ -40,6 +40,19 @@
     return jnp.concatenate([gate_grad, up_grad], axis=1).astype(jnp.bfloat16)
 
 
+def dp_sum(part):
+    if lax.axis_size("dp") == 2:
+        other = lax.ppermute(part, "dp", [(0, 1), (1, 0)])
+        return part.astype(jnp.float32) + other.astype(jnp.float32)
+    return lax.psum_scatter(part, "dp", scatter_dimension=0, tiled=True).astype(jnp.float32)
+
+
+def dp_spread(rows):
+    if lax.axis_size("dp") == 2:
+        return rows
+    return lax.all_gather(rows, "dp", axis=0, tiled=True)
+
+
 def body(tokens, cotangent, routing, gate_values, hidden_weight, output_weight):
     tok_count, column_width = tokens.shape
     pick_count = routing.shape[1]
@@ -70,29 +83,19 @@
     )
     expert_rows = arrived[0].reshape(row_total, column_width)
     scaled_cot = arrived[1].reshape(row_total, column_width)
-    picked_rows = expert_rows
-    hidden = lax.psum_scatter(
-        jnp.dot(picked_rows, inner_weight, preferred_element_type=jnp.float32).astype(jnp.bfloat16),
-        "dp",
-        scatter_dimension=0,
-        tiled=True,
-    ).astype(jnp.float32)
-    active = lax.all_gather(activate(hidden, half_width), "dp", axis=0, tiled=True)
+    hidden_part = jnp.dot(
+        expert_rows, inner_weight, preferred_element_type=jnp.float32
+    ).astype(jnp.bfloat16)
+    hidden = dp_sum(hidden_part)
+    active = dp_spread(activate(hidden, half_width))
     expert_out = jnp.dot(active, outer_weight, preferred_element_type=jnp.float32).astype(
         jnp.bfloat16
     )
-    picked_rows = scaled_cot
-    act_part = lax.psum_scatter(
-        lax.dot_general(
-            picked_rows, outer_weight, contract_cols, preferred_element_type=jnp.float32
-        ).astype(jnp.bfloat16),
-        "dp",
-        scatter_dimension=0,
-        tiled=True,
-    ).astype(jnp.float32)
-    hidden_cot = lax.all_gather(
-        activate_grad(hidden, act_part, half_width), "dp", axis=0, tiled=True
-    )
+    expert_out, late_cot = lax.optimization_barrier((expert_out, scaled_cot))
+    act_part = lax.dot_general(
+        late_cot, outer_weight, contract_cols, preferred_element_type=jnp.float32
+    ).astype(jnp.bfloat16)
+    hidden_cot = dp_spread(activate_grad(hidden, dp_sum(act_part), half_width))
     output_grad = lax.dot_general(
         active, scaled_cot, contract_rows, preferred_element_type=jnp.float32
     ).astype(jnp.bfloat16)

time: 255 us -> 203 us (0.80)
  waiting for transfers between devices: 137 us -> 104 us
  between operations: 13.9 us -> 0.78 us
  blocking collectives: 7.71 us -> 0 us
  matrix products: 59.7 us -> 63.4 us
    ppermute x0 -> x2, waiting for transfers between devices: none -> 35.2 us  [dp_sum(): other = lax.ppermute(part, 'dp', [(0, 1), (1, 0)])]
    all_to_all x1, waiting for transfers between devices: 33.3 us -> 2.81 us  [body(): lax.all_to_all(cot_rows, 'expert', split_axis=0, concat_axis=0, tiled=True)]
    all_gather x1 -> x0, waiting for transfers between devices: 22.7 us -> none  [body(): lax.all_gather(activate_grad(hidden, act_part, half_width), 'dp', axis=0,...]
    reduce_scatter x2 -> x0, waiting for transfers between devices: 12.9 us -> none  [the longest x1 12.9 us: body(): lax.psum_scatter(lax.dot_general(picked_rows, outer_weight, contract_cols...]
    all_gather x1 -> x0, blocking collectives: 7.71 us -> none  [body(): lax.all_gather(activate(hidden, half_width), 'dp', axis=0, tiled=True)]
    dot_general x1, matrix products: 10.8 us -> 16.1 us  [body(): lax.dot_general(hidden_cot, inner_weight, contract_cols, preferred_elemen...]
    ppermute x0 -> x2, starting transfers between devices: none -> 2.55 us  [dp_sum(): other = lax.ppermute(part, 'dp', [(0, 1), (1, 0)])]
  transfers between devices with their start and end apart: 7 -> 6, of which waited for: 6 -> 6; matrix products, arithmetic and copies ran while one was open for 20% -> 30% of each run, Pallas kernels for 0% -> 0%
where the time goes in v1:
time: 203 us
  waiting for transfers between devices  104 us (51%)
  matrix products  63.4 us (31%)
  starting transfers between devices  23.5 us (12%)
  other arithmetic  8.75 us (4%)
  local copies, waits for them, and re-layouts  2.58 us (1%)
    all_to_all x1, waiting for transfers between devices, body(): lax.all_to_all(token_rows, 'expert', split_axis=0, concat_axis=0, tiled=T...  37.4 us
    ppermute x2, waiting for transfers between devices, dp_sum(): other = lax.ppermute(part, 'dp', [(0, 1), (1, 0)])  35.2 us
    all_to_all x1, waiting for transfers between devices, body(): lax.all_to_all(row_grad.reshape(send_shape), 'expert', split_axis=0, conc...  22.9 us
    dot_general x1, matrix products, body(): lax.dot_general(hidden_cot, inner_weight, contract_cols, preferred_elemen...  16.1 us
    dot_general x1, matrix products, body(): lax.dot_general(expert_rows, hidden_cot, contract_rows, preferred_element...  7.63 us
    dot_general x1, matrix products, body(): jnp.dot(expert_rows, inner_weight, preferred_element_type=jnp.float32)  7.55 us
    dot_general x1, matrix products, body(): lax.dot_general(active, scaled_cot, contract_rows, preferred_element_type...  6.81 us
    all_to_all x1, starting transfers between devices, body(): lax.all_to_all(token_rows, 'expert', split_axis=0, concat_axis=0, tiled=T...  6.65 us
  transfers between devices with their start and end apart: 6, of which 6 were waited for; matrix products, arithmetic and copies ran while one was open for 30% of the time, Pallas kernels for 0%

profile of v1, /device:TPU:13, one launch (start us, length us, event | category | flops | bytes accessed | tf_op | source)
XLA Modules:
  0.0 202.7 jit_solution(2636322918301764352)
XLA Ops:
  0.6 1.0 copy.22
  1.9 4.5 %reduce-window.6 = s32[16,16,128]{2,1,0:T(8,128)S(1)} reduce-window(s32[16,16,128]{2,1,0:T(8,128)S(1)} %fusion.30, s32[]{:T(128)} %constant.6.clone.1), window={size=1x1x128 pad=0_0x0_0x127_0}, to_apply=%region_0.0 | reduce-window | flops 4161536 | bytes 262148 | tf_op jit(solution)/shard_map/reduce-window
  6.4 0.4 slice_reduce_fusion
  7.3 0.7 multiply_add_fusion
  8.1 0.9 fusion.20
  8.9 1.9 convolution_convert_fusion.4
  10.8 6.7 %all-to-all-start = ((bf16[16,16,3584]{2,1,0:T(8,128)(2,1)}), bf16[16,16,3584]{2,1,0:T(8,128)(2,1)S(1)}, u32[]{:S(2)}, u32[]{:S(2)}) async-start(bf16[16,16,3584]{2,1,0:T(8,128)(2,1)} %bitcast.60), calls=%async_computation | async-start | bytes 3670016 | tf_op jit(solution)/shard_map/all_to_all | solution.py:81
  17.5 1.0 select_reduce_fusion
  18.5 3.4 %fusion.16 = bf16[256,3584]{1,0:T(8,128)(2,1)} fusion(bf16[256,3584]{1,0:T(8,128)(2,1)} %param.7, f32[256]{0:T(256)S(1)} %select_reduce_fusion, pred[256,256]{1,0:T(8,128)(4,1)S(1)} %fusion.20), kind=kOutput, calls=%fused_computation.15 | convolution fusion | flops 471728128 | bytes 3736576 | tf_op jit(solution)/shard_map/dot_general | solution.py:73
  21.9 37.4 %all-to-all-done = bf16[16,16,3584]{2,1,0:T(8,128)(2,1)S(1)} async-done(((bf16[16,16,3584]{2,1,0:T(8,128)(2,1)}), bf16[16,16,3584]{2,1,0:T(8,128)(2,1)S(1)}, u32[]{:S(2)}, u32[]{:S(2)}) %all-to-all-start) | async-done | bytes 1835040 | tf_op jit(solution)/shard_map/all_to_all | solution.py:81
  59.3 4.8 %all-to-all-start.1 = ((bf16[16,16,3584]{2,1,0:T(8,128)(2,1)}), bf16[16,16,3584]{2,1,0:T(8,128)(2,1)}, u32[]{:S(2)}, u32[]{:S(2)}) async-start(bf16[16,16,3584]{2,1,0:T(8,128)(2,1)} %bitcast.61), calls=%async_computation.1 | async-start | bytes 3670016 | tf_op jit(solution)/shard_map/all_to_all | solution.py:82
  64.1 7.5 %fusion.17 = bf16[256,2048]{1,0:T(8,128)(2,1)S(1)} fusion(bf16[256,3584]{1,0:T(8,128)(2,1)S(1)} %bitcast.58, bf16[1,3584,2048]{2,1,0:T(8,128)(2,1)} %param.10), kind=kOutput, calls=%fused_computation.19 | convolution fusion | flops 3758620672 | bytes 17563648 | tf_op jit(solution)/shard_map/dot_general | solution.py:86
  71.6 1.3 collective-permute-start
  72.9 23.2 %collective-permute-done = bf16[256,2048]{1,0:T(8,128)(2,1)S(1)} collective-permute-done((bf16[256,2048]{1,0:T(8,128)(2,1)S(1)}, bf16[256,2048]{1,0:T(8,128)(2,1)S(1)}, u32[]{:S(2)}, u32[]{:S(2)}) %collective-permute-start) | collective-permute-done | bytes 1048608 | tf_op jit(solution)/shard_map/ppermute | solution.py:45
  96.1 0.3 convert_add_fusion
  96.5 0.3 multiply_convert_fusion.2
  96.8 6.4 %fusion.10 = bf16[256,3584]{1,0:T(8,128)(2,1)} fusion(bf16[256,1024]{1,0:T(8,128)(2,1)S(1)} %multiply_convert_fusion.2, bf16[1,1024,3584]{2,1,0:T(8,128)(2,1)} %param.11), kind=kOutput, calls=%fused_computation.13 | convolution fusion | flops 1879965696 | bytes 9699328 | tf_op jit(solution)/shard_map/dot_general | solution.py:91
  103.2 2.8 %all-to-all-done.1 = bf16[16,16,3584]{2,1,0:T(8,128)(2,1)} async-done(((bf16[16,16,3584]{2,1,0:T(8,128)(2,1)}), bf16[16,16,3584]{2,1,0:T(8,128)(2,1)}, u32[]{:S(2)}, u32[]{:S(2)}) %all-to-all-start.1) | async-done | bytes 1835040 | tf_op jit(solution)/shard_map/all_to_all | solution.py:82
  106.0 4.8 %all-to-all-start.2 = ((bf16[16,16,3584]{2,1,0:T(8,128)(2,1)}), bf16[16,16,3584]{2,1,0:T(8,128)(2,1)}, u32[]{:S(2)}, u32[]{:S(2)}) async-start(bf16[16,16,3584]{2,1,0:T(8,128)(2,1)} %bitcast.62), calls=%async_computation.2 | async-start | bytes 3670016 | tf_op jit(solution)/shard_map/all_to_all | solution.py:109
  110.7 5.7 %fusion.21 = bf16[256,1024]{1,0:T(8,128)(2,1)S(1)} fusion(bf16[256,3584]{1,0:T(8,128)(2,1)} %bitcast.6, bf16[1,1024,3584]{2,1,0:T(8,128)(2,1)} %param.11), kind=kOutput, calls=%fused_computation.24 | convolution fusion | flops 1879310336 | bytes 9699328 | tf_op jit(solution)/shard_map/dot_general | solution.py:95
  116.5 1.3 collective-permute-start.1
  117.8 12.0 %collective-permute-done.1 = bf16[256,1024]{1,0:T(8,128)(2,1)S(1)} collective-permute-done((bf16[256,1024]{1,0:T(8,128)(2,1)S(1)}, bf16[256,1024]{1,0:T(8,128)(2,1)S(1)}, u32[]{:S(2)}, u32[]{:S(2)}) %collective-permute-start.1) | collective-permute-done | bytes 524320 | tf_op jit(solution)/shard_map/ppermute | solution.py:45
  129.7 0.6 multiply_convert_fusion.1
  130.3 0.8 copy-done.4
  131.1 16.1 %fusion.13 = bf16[256,3584]{1,0:T(8,128)(2,1)} fusion(bf16[1,3584,2048]{2,1,0:T(8,128)(2,1)} %param.10, bf16[256,1024]{1,0:T(8,128)(2,1)S(1)} %get-tuple-element.9, bf16[256,1024]{1,0:T(8,128)(2,1)S(1)} %get-tuple-element.8), kind=kOutput, calls=%fused_computation.14 | convolution fusion | flops 3761111040 | bytes 17563648 | tf_op jit(solution)/shard_map/dot_general | solution.py:105
  147.3 5.4 %all-to-all-done.2 = bf16[16,16,3584]{2,1,0:T(8,128)(2,1)} async-done(((bf16[16,16,3584]{2,1,0:T(8,128)(2,1)}), bf16[16,16,3584]{2,1,0:T(8,128)(2,1)}, u32[]{:S(2)}, u32[]{:S(2)}) %all-to-all-start.2) | async-done | bytes 1835040 | tf_op jit(solution)/shard_map/all_to_all | solution.py:109
  152.6 4.8 %all-to-all-start.3 = ((bf16[16,16,3584]{2,1,0:T(8,128)(2,1)}), bf16[16,16,3584]{2,1,0:T(8,128)(2,1)}, u32[]{:S(2)}, u32[]{:S(2)}) async-start(bf16[16,16,3584]{2,1,0:T(8,128)(2,1)} %bitcast.9), calls=%async_computation.3 | async-start | bytes 3670016 | tf_op jit(solution)/shard_map/all_to_all | solution.py:112
  157.4 6.8 %fusion.9 = bf16[1,1024,3584]{2,1,0:T(8,128)(2,1)} fusion(bf16[256,1024]{1,0:T(8,128)(2,1)S(1)} %multiply_convert_fusion.2, bf16[256,3584]{1,0:T(8,128)(2,1)} %bitcast.6), kind=kOutput, calls=%fused_computation.11 | convolution fusion | flops 1882718208 | bytes 9699328 | tf_op jit(solution)/shard_map/dot_general | solution.py:99
  164.3 7.6 %fusion.4 = bf16[1,3584,2048]{2,1,0:T(8,128)(2,1)} fusion(bf16[256,3584]{1,0:T(8,128)(2,1)S(1)} %bitcast.59, bf16[256,1024]{1,0:T(8,128)(2,1)S(1)} %copy-done.5, bf16[256,1024]{1,0:T(8,128)(2,1)S(1)} %get-tuple-element.8), kind=kOutput, calls=%fused_computation.5 | convolution fusion | flops 3767533568 | bytes 17563648 | tf_op jit(solution)/shard_map/dot_general | solution.py:102
  171.9 4.6 %convolution_convert_fusion.3 = bf16[256,3584]{1,0:T(8,128)(2,1)} fusion(bf16[256,3584]{1,0:T(8,128)(2,1)} %bitcast.8, pred[256,256]{1,0:T(8,128)(4,1)S(1)} %fusion.20, f32[256]{0:T(256)S(1)} %select_reduce_fusion), kind=kOutput, calls=%fused_computation.17 | convolution fusion | flops 2819555328 | bytes 3736576 | tf_op jit(solution)/shard_map/dot_general | solution.py:121
  176.5 22.9 %all-to-all-done.3 = bf16[16,16,3584]{2,1,0:T(8,128)(2,1)} async-done(((bf16[16,16,3584]{2,1,0:T(8,128)(2,1)}), bf16[16,16,3584]{2,1,0:T(8,128)(2,1)}, u32[]{:S(2)}, u32[]{:S(2)}) %all-to-all-start.3) | async-done | bytes 1835040 | tf_op jit(solution)/shard_map/all_to_all | solution.py:112
  199.3 3.4 %convolution_convert_fusion.2 = bf16[256,3584]{1,0:T(8,128)(2,1)} fusion(bf16[256,3584]{1,0:T(8,128)(2,1)} %bitcast.10, pred[256,256]{1,0:T(8,128)(4,1)S(1)} %fusion.20), kind=kOutput, calls=%fused_computation.16 | convolution fusion | flops 470810624 | bytes 3735552 | tf_op jit(solution)/shard_map/dot_general | solution.py:128
  (21 shorter events, 0.8 us)
Async XLA Ops:
  0.6 8.3 %copy-start = (bf16[256,3584]{1,0:T(8,128)(2,1)S(1)}, bf16[256,3584]{1,0:T(8,128)(2,1)}, u32[]{:S(2)}) copy-start(bf16[256,3584]{1,0:T(8,128)(2,1)} %param.6) | copy-start | bytes 5505028
  10.8 6.7 %copy-start.6 = (f32[256,8]{0,1:T(8,128)S(1)}, f32[256,8]{0,1:T(8,128)}, u32[]{:S(2)}) copy-start(f32[256,8]{0,1:T(8,128)} %param.9) | copy-start | bytes 24580
  10.8 48.5 %all-to-all-start = ((bf16[16,16,3584]{2,1,0:T(8,128)(2,1)}), bf16[16,16,3584]{2,1,0:T(8,128)(2,1)S(1)}, u32[]{:S(2)}, u32[]{:S(2)}) async-start(bf16[16,16,3584]{2,1,0:T(8,128)(2,1)} %bitcast.60), calls=%async_computation | async-start | bytes 3670016 | tf_op jit(solution)/shard_map/all_to_all | solution.py:81
  59.3 12.3 %copy-start.2 = (bf16[16,16,3584]{2,1,0:T(8,128)(2,1)}, bf16[16,16,3584]{2,1,0:T(8,128)(2,1)S(1)}, u32[]{:S(2)}) copy-start(bf16[16,16,3584]{2,1,0:T(8,128)(2,1)S(1)} %all-to-all-done) | copy-start | bytes 5505028
  59.3 46.7 %all-to-all-start.1 = ((bf16[16,16,3584]{2,1,0:T(8,128)(2,1)}), bf16[16,16,3584]{2,1,0:T(8,128)(2,1)}, u32[]{:S(2)}, u32[]{:S(2)}) async-start(bf16[16,16,3584]{2,1,0:T(8,128)(2,1)} %bitcast.61), calls=%async_computation.1 | async-start | bytes 3670016 | tf_op jit(solution)/shard_map/all_to_all | solution.py:82
  71.6 24.5 %collective-permute-start = (bf16[256,2048]{1,0:T(8,128)(2,1)S(1)}, bf16[256,2048]{1,0:T(8,128)(2,1)S(1)}, u32[]{:S(2)}, u32[]{:S(2)}) collective-permute-start(bf16[256,2048]{1,0:T(8,128)(2,1)S(1)} %fusion.17), channel_id=1, source_target_pairs={{0,16},{16,0},{1,17},{17,1},{2,18},{18,2},{3,19},{19,3},{4,20},{20... | collective-permute-start | bytes 3145736 | tf_op jit(solution)/shard_map/ppermute | solution.py:45
  106.0 46.7 %all-to-all-start.2 = ((bf16[16,16,3584]{2,1,0:T(8,128)(2,1)}), bf16[16,16,3584]{2,1,0:T(8,128)(2,1)}, u32[]{:S(2)}, u32[]{:S(2)}) async-start(bf16[16,16,3584]{2,1,0:T(8,128)(2,1)} %bitcast.62), calls=%async_computation.2 | async-start | bytes 3670016 | tf_op jit(solution)/shard_map/all_to_all | solution.py:109
  116.5 13.3 %collective-permute-start.1 = (bf16[256,1024]{1,0:T(8,128)(2,1)S(1)}, bf16[256,1024]{1,0:T(8,128)(2,1)S(1)}, u32[]{:S(2)}, u32[]{:S(2)}) collective-permute-start(bf16[256,1024]{1,0:T(8,128)(2,1)S(1)} %fusion.21), channel_id=1, source_target_pairs={{0,16},{16,0},{1,17},{17,1},{2,18},{18,2},{3,19},{19,3},{4,20},{20... | collective-permute-start | bytes 1572872 | tf_op jit(solution)/shard_map/ppermute | solution.py:45
  130.3 0.8 copy-start.4
  152.6 46.7 %all-to-all-start.3 = ((bf16[16,16,3584]{2,1,0:T(8,128)(2,1)}), bf16[16,16,3584]{2,1,0:T(8,128)(2,1)}, u32[]{:S(2)}, u32[]{:S(2)}) async-start(bf16[16,16,3584]{2,1,0:T(8,128)(2,1)} %bitcast.9), calls=%async_computation.3 | async-start | bytes 3670016 | tf_op jit(solution)/shard_map/all_to_all | solution.py:112
  157.4 6.8 %copy-start.3 = (bf16[16,16,3584]{2,1,0:T(8,128)(2,1)S(1)}, bf16[16,16,3584]{2,1,0:T(8,128)(2,1)}, u32[]{:S(2)}) copy-start(bf16[16,16,3584]{2,1,0:T(8,128)(2,1)} %copy-done.2) | copy-start | bytes 5505028
  157.4 6.8 %copy-start.5 = (bf16[256,1024]{1,0:T(8,128)(2,1)S(1)}, bf16[256,1024]{1,0:T(8,128)(2,1)}, u32[]{:S(2)}) copy-start(bf16[256,1024]{1,0:T(8,128)(2,1)} %copy-done.4) | copy-start | bytes 1572868
  171.9 30.8 %copy-start.1 = (bf16[256,3584]{1,0:T(8,128)(2,1)S(1)}, bf16[256,3584]{1,0:T(8,128)(2,1)}, u32[]{:S(2)}) copy-start(bf16[256,3584]{1,0:T(8,128)(2,1)} %param.6) | copy-start | bytes 5505028

commit v2 on v1

v2 whole, which is shorter than its diff:
```python
import functools

import jax
import jax.numpy as jnp
from jax import lax
from jax.experimental import pallas as pl
from jax.experimental.pallas import tpu as pltpu
from jax.sharding import PartitionSpec as P


ROUTED = 256
VMEM_BYTES = 16 * 1024 * 1024


def slot_keys(route_ref, expert_ids):
    tok_count = route_ref.shape[1]
    chosen = route_ref[0:1, :] == expert_ids
    for k in range(1, route_ref.shape[0]):
        chosen = jnp.logical_or(chosen, route_ref[k : k + 1, :] == expert_ids)
    before = lax.broadcasted_iota(jnp.int32, (tok_count, tok_count), 0) < (
        lax.broadcasted_iota(jnp.int32, (tok_count, tok_count), 1)
    )
    rank = jnp.dot(
        chosen.astype(jnp.bfloat16), before.astype(jnp.bfloat16), preferred_element_type=jnp.float32
    )
    return jnp.where(chosen, rank.astype(jnp.int32), -1)


def expert_gates(route_ref, gate_ref, expert_ids):
    total = jnp.where(route_ref[0:1, :] == expert_ids, gate_ref[0:1, :], 0.0)
    for k in range(1, route_ref.shape[0]):
        total = total + jnp.where(route_ref[k : k + 1, :] == expert_ids, gate_ref[k : k + 1, :], 0.0)
    return total


def tile_width(width, limit):
    fits = [w for w in range(128, limit + 1, 128) if width % w == 0]
    return fits[-1] if fits else width


def experts_at(expert_count, tok_count, outer, own):
    at = lax.broadcasted_iota(jnp.int32, (expert_count, tok_count), 0)
    if outer > 1:
        shift = outer.bit_length() - 1
        at = (at & (outer - 1)) * (expert_count // outer) + lax.shift_right_logical(at, shift)
    return at ^ own


def gather_kernel(scaled, slot_count, outer, held, own_ref, route_ref, gate_ref, rows_ref, *refs):
    refs = refs[held:]
    out_refs, (placed_ref, gain_ref) = refs[:-2], refs[-2:]
    row_total, tok_count = placed_ref.shape
    expert_count, piece_rows = row_total // slot_count, out_refs[0].shape[0]

    @pl.when(pl.program_id(0) == 0)
    def _():
        expert_ids = experts_at(expert_count, tok_count, outer, own_ref[0])
        keys = slot_keys(route_ref, expert_ids)
        slots = lax.broadcasted_iota(jnp.int32, (slot_count, tok_count), 0)
        if scaled:
            gates = expert_gates(route_ref, gate_ref, expert_ids)
        for e in range(expert_count):
            here = pl.ds(e * slot_count, slot_count)
            matched = keys[e : e + 1, :] == slots
            placed_ref[here, :] = matched.astype(jnp.float32).astype(jnp.bfloat16)
            if scaled:
                gain_ref[here, :] = jnp.sum(
                    jnp.where(matched, gates[e : e + 1, :], 0.0), axis=1, keepdims=True
                )

    picked = jnp.dot(placed_ref[...], rows_ref[...], preferred_element_type=jnp.float32)
    if scaled:
        picked = gain_ref[...] * picked
    picked = picked.astype(jnp.bfloat16)
    for e, out_ref in enumerate(out_refs):
        out_ref[...] = picked[e * piece_rows : (e + 1) * piece_rows]


def gather_rows(own, routes, gates, rows, expert_count, slot_count, scaled, pieces, outer, held=()):
    tok_count, width = rows.shape
    row_total = expert_count * slot_count
    piece_rows = row_total // pieces
    block = tile_width(width, 1792)
    whole = pl.BlockSpec(routes.shape, lambda i: (0, 0))
    return pl.pallas_call(
        functools.partial(gather_kernel, scaled, slot_count, outer, len(held)),
        grid=(width // block,),
        in_specs=[
            pl.BlockSpec(memory_space=pltpu.SMEM),
            whole,
            whole,
            pl.BlockSpec((tok_count, block), lambda i: (0, i)),
        ]
        + [pl.BlockSpec(memory_space=pl.ANY)] * len(held),
        out_specs=[pl.BlockSpec((piece_rows, block), lambda i: (0, i))] * pieces,
        out_shape=[jax.ShapeDtypeStruct((piece_rows, width), jnp.bfloat16)] * pieces,
        scratch_shapes=[
            pltpu.VMEM((row_total, tok_count), jnp.bfloat16),
            pltpu.VMEM((row_total, 1), jnp.float32),
        ],
        compiler_params=pltpu.CompilerParams(vmem_limit_bytes=VMEM_BYTES if held else None),
        cost_estimate=pl.CostEstimate(
            flops=2 * row_total * tok_count * width,
            bytes_accessed=2 * (tok_count + row_total) * width,
            transcendentals=0,
        ),
    )(own, routes, gates, rows, *held)


def combine_kernel(weighted, expert_count, outer, own_ref, route_ref, gate_ref, *refs):
    row_refs, (out_ref, weight_ref) = refs[:-2], refs[-2:]
    row_total, tok_count = weight_ref.shape[-2:]
    slot_count = row_total // expert_count

    @pl.when(pl.program_id(0) == 0)
    def _():
        expert_ids = experts_at(expert_count, tok_count, outer, own_ref[0])
        keys = slot_keys(route_ref, expert_ids)
        slots = lax.broadcasted_iota(jnp.int32, (slot_count, tok_count), 0)
        if weighted:
            gates = expert_gates(route_ref, gate_ref, expert_ids)
        for e in range(expert_count):
            here = pl.ds(e * slot_count, slot_count)
            matched = keys[e : e + 1, :] == slots
            if not weighted:
                weight_ref[0, here, :] = matched.astype(jnp.float32).astype(jnp.bfloat16)
                continue
            left = jnp.where(matched, gates[e : e + 1, :], 0.0)
            for part in range(weight_ref.shape[0]):
                term = left.astype(jnp.bfloat16)
                weight_ref[part, here, :] = term
                left = left - term.astype(jnp.float32)

    rows = jnp.concatenate([ref[...] for ref in row_refs]) if row_refs[1:] else row_refs[0][...]
    total = None
    for part in range(weight_ref.shape[0]):
        term = lax.dot_general(
            weight_ref[part], rows, (((0,), (0,)), ((), ())), preferred_element_type=jnp.float32
        )
        total = term if total is None else total + term
    out_ref[...] = total.astype(jnp.bfloat16)


def combine_rows(own, routes, gates, pieces, expert_count, weighted, outer):
    tok_count = routes.shape[1]
    row_total, width = sum(piece.shape[0] for piece in pieces), pieces[0].shape[1]
    block = tile_width(width, 896)
    whole = pl.BlockSpec(routes.shape, lambda i: (0, 0))
    parts = 3 if weighted else 1
    return pl.pallas_call(
        functools.partial(combine_kernel, weighted, expert_count, outer),
        grid=(width // block,),
        in_specs=[pl.BlockSpec(memory_space=pltpu.SMEM), whole, whole]
        + [pl.BlockSpec((piece.shape[0], block), lambda i: (0, i)) for piece in pieces],
        out_specs=pl.BlockSpec((tok_count, block), lambda i: (0, i)),
        out_shape=jax.ShapeDtypeStruct((tok_count, width), jnp.bfloat16),
        scratch_shapes=[pltpu.VMEM((parts, row_total, tok_count), jnp.bfloat16)],
        compiler_params=pltpu.CompilerParams(vmem_limit_bytes=VMEM_BYTES),
        cost_estimate=pl.CostEstimate(
            flops=2 * parts * row_total * tok_count * width,
            bytes_accessed=2 * (tok_count + row_total) * width,
            transcendentals=0,
        ),
    )(own, routes, gates, *pieces)


def activate(hidden, half_width):
    gate_part = hidden[:, :half_width]
    up_part = hidden[:, half_width:]
    return (gate_part * jax.nn.sigmoid(gate_part) * up_part).astype(jnp.bfloat16)


def activate_grad(hidden, act_grad, half_width):
    gate_part = hidden[:, :half_width]
    up_part = hidden[:, half_width:]
    sigmoid_gate = jax.nn.sigmoid(gate_part)
    gate_grad = act_grad * up_part * sigmoid_gate * (1.0 + gate_part * (1.0 - sigmoid_gate))
    up_grad = act_grad * gate_part * sigmoid_gate
    return jnp.concatenate([gate_grad, up_grad], axis=1).astype(jnp.bfloat16)


def hold_kernel(count, *refs):
    copies = [
        pltpu.make_async_copy(refs[k], refs[count + k], refs[2 * count].at[k]) for k in range(count)
    ]
    for copy in copies:
        copy.start()
    for copy in copies:
        copy.wait()


def hold(*arrays):
    count = len(arrays)
    return pl.pallas_call(
        functools.partial(hold_kernel, count),
        in_specs=[pl.BlockSpec(memory_space=pl.ANY)] * count,
        out_specs=[pl.BlockSpec(memory_space=pltpu.VMEM)] * count,
        out_shape=[pltpu.VMEM(a.shape, a.dtype) for a in arrays],
        scratch_shapes=[pltpu.SemaphoreType.DMA((count,))],
        compiler_params=pltpu.CompilerParams(vmem_limit_bytes=VMEM_BYTES),
        cost_estimate=pl.CostEstimate(
            flops=0, bytes_accessed=4 * sum(a.size for a in arrays), transcendentals=0
        ),
    )(*arrays)


def column_kernel(first, left_ref, right_ref, out_ref):
    width = out_ref.shape[1]
    out_ref[...] = jnp.dot(
        left_ref[...], right_ref[:, first : first + width], preferred_element_type=jnp.float32
    ).astype(jnp.bfloat16)


def part_product(kernel, left, right, first, width):
    row_total, depth = left.shape
    return pl.pallas_call(
        functools.partial(kernel, first),
        in_specs=[pl.BlockSpec(memory_space=pltpu.VMEM)] * 2,
        out_specs=pl.BlockSpec(memory_space=pltpu.VMEM),
        out_shape=jax.ShapeDtypeStruct((row_total, width), jnp.bfloat16),
        compiler_params=pltpu.CompilerParams(vmem_limit_bytes=VMEM_BYTES),
        cost_estimate=pl.CostEstimate(
            flops=2 * row_total * depth * width,
            bytes_accessed=2 * (row_total + width) * depth + 2 * row_total * width,
            transcendentals=0,
        ),
    )(left, right)


def held_kernel(right_dim, block, groups, left_ref, right_ref, *out_refs):
    here = pl.ds(pl.multiple_of(pl.program_id(0) * block, block), block)
    right = right_ref[here, :] if right_dim == 1 else right_ref[:, here]
    rows = lax.dot_general(
        left_ref[...], right, (((1,), (right_dim,)), ((), ())), preferred_element_type=jnp.float32
    ).astype(jnp.bfloat16)
    run = rows.shape[0] // (len(out_refs) * groups)
    for p, out_ref in enumerate(out_refs):
        for g in range(groups):
            first = (g * len(out_refs) + p) * run
            out_ref[g * run : (g + 1) * run, :] = rows[first : first + run]


def held_product(left, right, right_dim, limit, pieces, groups):
    row_total, depth = left.shape
    width = right.shape[1 - right_dim]
    block = tile_width(width, limit)
    piece_rows = row_total // pieces
    return pl.pallas_call(
        functools.partial(held_kernel, right_dim, block, groups),
        grid=(width // block,),
        in_specs=[
            pl.BlockSpec((row_total, depth), lambda i: (0, 0)),
            pl.BlockSpec(memory_space=pltpu.VMEM),
        ],
        out_specs=[pl.BlockSpec((piece_rows, block), lambda i: (0, i))] * pieces,
        out_shape=[jax.ShapeDtypeStruct((piece_rows, width), jnp.bfloat16)] * pieces,
        compiler_params=pltpu.CompilerParams(vmem_limit_bytes=VMEM_BYTES),
        cost_estimate=pl.CostEstimate(
            flops=2 * row_total * depth * width,
            bytes_accessed=2 * (row_total + width) * depth + 2 * row_total * width,
            transcendentals=0,
        ),
    )(left, right)


def cot_kernel(first, left_ref, right_ref, out_ref):
    width = out_ref.shape[1]
    out_ref[...] = lax.dot_general(
        left_ref[...],
        right_ref[first : first + width, :],
        (((1,), (1,)), ((), ())),
        preferred_element_type=jnp.float32,
    ).astype(jnp.bfloat16)


def trade(pieces, step):
    count = lax.axis_size("expert")
    got = list(pieces)
    for k in range(len(pieces) - 1, 0, -1):
        pairs = [(i, i ^ (k * step)) for i in range(count)]
        got[k] = lax.ppermute(pieces[k], "expert", pairs)
    return got


def regroup(pieces, parts):
    rows = pieces[0].shape[0] // parts
    return [jnp.concatenate([p[k * rows : (k + 1) * rows] for p in pieces]) for k in range(parts)]


def cut(rows, parts):
    size = rows.shape[0] // parts
    return [rows[k * size : (k + 1) * size] for k in range(parts)]


def send_back(out_pieces, inner):
    return trade(regroup(trade(out_pieces, inner), inner), 1)


def dp_swap(part):
    return lax.ppermute(part, "dp", [(0, 1), (1, 0)])


def dp_sum(part):
    return lax.psum_scatter(part, "dp", scatter_dimension=0, tiled=True).astype(jnp.float32)


def pair_sum(pairs):
    sums = [own.astype(jnp.float32) + other.astype(jnp.float32) for own, other in pairs]
    return sums[0] if len(sums) == 1 else jnp.concatenate(sums, axis=1)


def dp_spread(rows):
    if lax.axis_size("dp") == 2:
        return rows
    return lax.all_gather(rows, "dp", axis=0, tiled=True)


def middle_ring(expert_rows, scaled_cot, inner_weight, outer_weight, outer, inner):
    contract_cols = (((1,), (1,)), ((), ()))
    half_width = outer_weight.shape[0]
    part = jnp.dot(jnp.concatenate(expert_rows), inner_weight, preferred_element_type=jnp.float32)
    hidden = dp_sum(part.astype(jnp.bfloat16))
    active = dp_spread(activate(hidden, half_width))
    expert_out = jnp.dot(active, outer_weight, preferred_element_type=jnp.float32)
    out_pieces = cut(expert_out.astype(jnp.bfloat16), outer)
    back_out = send_back(out_pieces, inner)
    part = lax.dot_general(
        scaled_cot, outer_weight, contract_cols, preferred_element_type=jnp.float32
    )
    act_grad = dp_sum(part.astype(jnp.bfloat16))
    hidden_cot = dp_spread(activate_grad(hidden, act_grad, half_width))
    row_grad = lax.dot_general(
        hidden_cot, inner_weight, contract_cols, preferred_element_type=jnp.float32
    )
    grad_pieces = regroup(cut(row_grad.astype(jnp.bfloat16), outer), inner)
    return active, hidden_cot, back_out, grad_pieces


def middle_pair(expert_rows, scaled_cot, inner_weight, outer_weight, outer, inner):
    half_width = outer_weight.shape[0]
    inner_weight, outer_weight = hold(inner_weight, outer_weight)
    sides, actives, out_pieces = [], [], []
    for at, rows in enumerate(expert_rows):
        sides.append([])
        for side in range(2):
            part = part_product(column_kernel, rows, inner_weight, side * half_width, half_width)
            sides[at].append((part, dp_swap(part)))
    for at, side in enumerate(sides):
        actives.append(activate(pair_sum(side), half_width))
        out_pieces += held_product(actives[at], outer_weight, 0, 512, outer // 2, 1)
    active = jnp.concatenate(actives)
    own_piece, late_sides = lax.optimization_barrier((out_pieces[0], sides))
    back_out = send_back([own_piece, *out_pieces[1:]], inner)

    chunk = half_width // CHUNKS
    pairs = []
    for at in range(CHUNKS):
        part = part_product(cot_kernel, scaled_cot, outer_weight, at * chunk, chunk)
        pairs.append((part, dp_swap(part)))
    hidden = jnp.concatenate([pair_sum(side) for side in late_sides])
    hidden_cot = activate_grad(hidden, pair_sum(pairs), half_width)
    grad_pieces = held_product(hidden_cot, inner_weight, 1, 512, inner, outer)
    return active, hidden_cot, back_out, grad_pieces


def body(tokens, cotangent, routing, gate_values, hidden_weight, output_weight):
    tok_count, _ = tokens.shape
    pick_count = routing.shape[1]
    expert_count = lax.axis_size("expert")
    slot_count = 2 * tok_count * pick_count // ROUTED
    contract_rows = (((0,), (0,)), ((), ()))
    outer = 1 << ((expert_count.bit_length() - 1) // 2)
    inner = expert_count // outer
    own = lax.axis_index("expert").astype(jnp.int32)
    routes, gates = routing.T, gate_values.T
    inner_weight = hidden_weight[0]
    outer_weight = output_weight[0]
    table = (routes, gates)

    mine = own[None]
    token_pieces = gather_rows(
        mine, *table, tokens, expert_count, slot_count, False, outer, 1
    )
    moved = trade(token_pieces, inner)
    expert_rows = []
    for run in (moved[: outer // 2], moved[outer // 2 :]):
        run = regroup(run, inner)
        run = trade(run, 1)
        expert_rows.append(jnp.concatenate(regroup(run, outer // 2)))

    cot = gather_rows(mine, *table, cotangent, expert_count, slot_count, True, inner, outer)
    cot = trade(cot, 1)
    cot = regroup(cot, outer)
    scaled_cot = jnp.concatenate(trade(cot, inner))

    middle = middle_pair if lax.axis_size("dp") == 2 else middle_ring
    active, hidden_cot, back_out, grad_pieces = middle(
        expert_rows, scaled_cot, inner_weight, outer_weight, outer, inner
    )
    grad_pieces = trade(grad_pieces, 1)
    grad_pieces = regroup(grad_pieces, outer)
    back_grad = trade(grad_pieces, inner)

    output_grad = lax.dot_general(
        active, scaled_cot, contract_rows, preferred_element_type=jnp.float32
    ).astype(jnp.bfloat16)
    hidden_grad = lax.dot_general(
        jnp.concatenate(expert_rows), hidden_cot, contract_rows, preferred_element_type=jnp.float32
    ).astype(jnp.bfloat16)
    mixed = combine_rows(mine, *table, back_out, expert_count, True, outer)
    token_grad = combine_rows(mine, *table, back_grad, expert_count, False, 1)
    return (mixed, token_grad, hidden_grad[None], output_grad[None])


CHUNKS = 2


def solution(mesh):
    return jax.shard_map(
        body,
        mesh=mesh,
        in_specs=(
            P("expert", "dp"),
            P("expert", "dp"),
            P("expert", None),
            P("expert", None),
            P("expert", "dp", None),
            P("expert", None, "dp"),
        ),
        out_specs=(
            P("expert", "dp"),
            P("expert", "dp"),
            P("expert", "dp", None),
            P("expert", None, "dp"),
        ),
        check_vma=False,
    )
```

time: 203 us -> 222 us (1.094)
  matrix products: 63.4 us -> 14.3 us
  Pallas kernels: 0 us -> 35.2 us
  starting transfers between devices: 23.5 us -> 53.4 us
  other arithmetic: 8.75 us -> 2.36 us
  local copies, waits for them, and re-layouts: 2.58 us -> 7.98 us
    ppermute x2 -> x33, waiting for transfers between devices: 35.2 us -> 105 us  [the longest x27 86.8 us: trade(): got[k] = lax.ppermute(pieces[k], 'expert', pairs)]
    all_to_all x4 -> x0, waiting for transfers between devices: 68.5 us -> none  [the longest x1 37.4 us: body(): lax.all_to_all(token_rows, 'expert', split_axis=0, concat_axis=0, tiled=T...]
    ppermute x2 -> x33, starting transfers between devices: 2.55 us -> 53.4 us  [the longest x27 47.8 us: trade(): got[k] = lax.ppermute(pieces[k], 'expert', pairs)]
    dot_general x9 -> x1, matrix products: 56.6 us -> 9.12 us  [body(): lax.dot_general(jnp.concatenate(expert_rows), hidden_cot, contract_rows,...]
    pallas_call x0 -> x14, Pallas kernels: none -> 35.2 us  [the longest x3 10.2 us: held_product(): pl.pallas_call(functools.partial(held_kernel, right_dim, block, groups),...]
    all_to_all x4 -> x0, starting transfers between devices: 21 us -> none  [the longest x1 6.65 us: body(): lax.all_to_all(token_rows, 'expert', split_axis=0, concat_axis=0, tiled=T...]
    another operation x4 -> x1, other arithmetic: 5.42 us -> 0.7 us
    slice x1 -> x14, local copies, waits for them, and re-layouts: 0.43 us -> 4.36 us  [regroup(): p[k * rows:(k + 1) * rows]]
  transfers between devices with their start and end apart: 6 -> 33, of which waited for: 6 -> 15; matrix products, arithmetic and copies ran while one was open for 30% -> 10% of each run, Pallas kernels for 0% -> 13%
where the time goes in v2:
time: 222 us; the launch traced here: 220 us
  waiting for transfers between devices  105 us (47%)
  starting transfers between devices  53.4 us (24%)
  Pallas kernels  35.2 us (16%)
  matrix products  14.3 us (6%)
  local copies, waits for them, and re-layouts  7.98 us (4%)
  other arithmetic  2.36 us (1%)
    ppermute x27, waiting for transfers between devices, trade(): got[k] = lax.ppermute(pieces[k], 'expert', pairs)  86.8 us
    ppermute x27, starting transfers between devices, trade(): got[k] = lax.ppermute(pieces[k], 'expert', pairs)  47.8 us
    ppermute x6, waiting for transfers between devices, dp_swap(): return lax.ppermute(part, 'dp', [(0, 1), (1, 0)])  18.4 us
    pallas_call x3, Pallas kernels, held_product(): pl.pallas_call(functools.partial(held_kernel, right_dim, block, groups),...  10.2 us
    dot_general x1, matrix products, body(): lax.dot_general(jnp.concatenate(expert_rows), hidden_cot, contract_rows,...  9.12 us
    pallas_call x6, Pallas kernels, part_product(): pl.pallas_call(functools.partial(kernel, first), in_specs=[pl.BlockSpec(m...  6.77 us
    pallas_call x2, Pallas kernels, combine_rows(): pl.pallas_call(functools.partial(combine_kernel, weighted, expert_count,...  6.62 us
    pallas_call x2, Pallas kernels, gather_rows(): pl.pallas_call(functools.partial(gather_kernel, scaled, slot_count, outer...  6.34 us
  transfers between devices with their start and end apart: 33, of which 15 were waited for; matrix products, arithmetic and copies ran while one was open for 10% of the time, Pallas kernels for 13%

profile of v2, /device:TPU:13, one launch (start us, length us, event | category | flops | bytes accessed | tf_op | source)
XLA Modules:
  0.0 219.7 jit_solution(5895114743711663531)
XLA Ops:
  0.6 3.1 %shard_map.93 = (bf16[64,3584]{1,0:T(8,128)(2,1)}, bf16[64,3584]{1,0:T(8,128)(2,1)}, bf16[64,3584]{1,0:T(8,128)(2,1)}, bf16[64,3584]{1,0:T(8,128)(2,1)}) custom-call(s32[1]{0:T(128)} %bitcast.own_ref, s32[8,256]{1,0:T(8,128)} %bitcast.12, f32[8,256]{1,0:T(8,128)} %bitcast.16, bf16[256,3584]{1,0:T(8,128)(2,1)} %rows_ref.2), custom_call_target="tpu_custom_call" | custom-call | flops 469762048 | bytes 3670016 | tf_op jit(solution)/shard_map/pallas_call | solution.py:85
  3.9 2.3 %collective-permute-start.6 = (bf16[64,3584]{1,0:T(8,128)(2,1)}, bf16[64,3584]{1,0:T(8,128)(2,1)S(1)}, u32[]{:S(2)}, u32[]{:S(2)}) collective-permute-start(bf16[64,3584]{1,0:T(8,128)(2,1)} %get-tuple-element.36), channel_id=1, source_target_pairs={{0,8},{1,9},{2,10},{3,11},{4,12},{5,13},{6,14},{7,15},{8,0},{9,1},... | collective-permute-start | bytes 1376264 | tf_op jit(solution)/shard_map/ppermute | solution.py:281
  6.4 3.2 %shard_map.102 = (bf16[64,3584]{1,0:T(8,128)(2,1)}, bf16[64,3584]{1,0:T(8,128)(2,1)}, bf16[64,3584]{1,0:T(8,128)(2,1)}, bf16[64,3584]{1,0:T(8,128)(2,1)}) custom-call(s32[1]{0:T(128)} %bitcast.own_ref, s32[8,256]{1,0:T(8,128)} %bitcast.13, f32[8,256]{1,0:T(8,128)} %bitcast.17, bf16[256,3584]{1,0:T(8,128)(2,1)} %rows_ref.3), custom_call_target="tpu_custom_call" | custom-call | flops 469762048 | bytes 3670016 | tf_op jit(solution)/shard_map/pallas_call | solution.py:85
  9.7 1.5 collective-permute-start.19
  11.5 3.1 %copy-done = bf16[1,1024,3584]{2,1,0:T(8,128)(2,1)S(1)} copy-done((bf16[1,1024,3584]{2,1,0:T(8,128)(2,1)S(1)}, bf16[1,1024,3584]{2,1,0:T(8,128)(2,1)}, u32[]{:S(2)}) %copy-start) | copy-done | bytes 7340056
  14.5 5.3 %shard_map.94 = (bf16[3584,2048]{1,0:T(8,128)(2,1)S(1)}, bf16[1024,3584]{1,0:T(8,128)(2,1)S(1)}) custom-call(bf16[3584,2048]{1,0:T(8,128)(2,1)} %bitcast.20, bf16[1024,3584]{1,0:T(8,128)(2,1)S(1)} %bitcast.11), custom_call_target="tpu_custom_call" | custom-call | bytes 44040192 | tf_op jit(solution)/shard_map/pallas_call | solution.py:194
  19.9 1.5 collective-permute-start.21
  21.4 1.9 collective-permute-done.20
  23.4 10.0 %collective-permute-done.21 = bf16[64,3584]{1,0:T(8,128)(2,1)S(1)} collective-permute-done((bf16[64,3584]{1,0:T(8,128)(2,1)S(1)}, bf16[64,3584]{1,0:T(8,128)(2,1)S(1)}, u32[]{:S(2)}, u32[]{:S(2)}) %collective-permute-start.21) | collective-permute-done | bytes 458784 | tf_op jit(solution)/shard_map/ppermute | solution.py:281
  33.5 1.4 collective-permute-start.22
  35.0 2.2 %collective-permute-start.23 = (bf16[64,3584]{1,0:T(8,128)(2,1)S(1)}, bf16[64,3584]{1,0:T(8,128)(2,1)S(1)}, u32[]{:S(2)}, u32[]{:S(2)}) collective-permute-start(bf16[64,3584]{1,0:T(8,128)(2,1)S(1)} %pad_maximum_fusion.7), channel_id=1, source_target_pairs={{0,8},{1,9},{2,10},{3,11},{4,12},{5,13},{6,14},{7,15},{8,0},{9,1},... | collective-permute-start | bytes 1376264 | tf_op jit(solution)/shard_map/ppermute | solution.py:281
  37.7 8.2 %collective-permute-done.7 = bf16[64,3584]{1,0:T(8,128)(2,1)S(1)} collective-permute-done((bf16[64,3584]{1,0:T(8,128)(2,1)}, bf16[64,3584]{1,0:T(8,128)(2,1)S(1)}, u32[]{:S(2)}, u32[]{:S(2)}) %collective-permute-start.7) | collective-permute-done | bytes 458784 | tf_op jit(solution)/shard_map/ppermute | solution.py:281
  45.9 22.8 %collective-permute-start.1 = (bf16[32,3584]{1,0:T(8,128)(2,1)S(1)}, bf16[32,3584]{1,0:T(8,128)(2,1)S(1)}, u32[]{:S(2)}, u32[]{:S(2)}) collective-permute-start(bf16[32,3584]{1,0:T(8,128)(2,1)S(1)} %pad_maximum_fusion.13), channel_id=1, source_target_pairs={{0,1},{1,0},{2,3},{3,2},{4,5},{5,4},{6,7},{7,6},{8,9},{9,8},{10,11... | collective-permute-start | bytes 688136 | tf_op jit(solution)/shard_map/ppermute | solution.py:281
  70.0 6.5 %collective-permute-done.2 = bf16[32,3584]{1,0:T(8,128)(2,1)S(1)} collective-permute-done((bf16[32,3584]{1,0:T(8,128)(2,1)S(1)}, bf16[32,3584]{1,0:T(8,128)(2,1)S(1)}, u32[]{:S(2)}, u32[]{:S(2)}) %collective-permute-start.2) | collective-permute-done | bytes 229408 | tf_op jit(solution)/shard_map/ppermute | solution.py:281
  77.9 6.3 %collective-permute-done.3 = bf16[32,3584]{1,0:T(8,128)(2,1)S(1)} collective-permute-done((bf16[32,3584]{1,0:T(8,128)(2,1)S(1)}, bf16[32,3584]{1,0:T(8,128)(2,1)S(1)}, u32[]{:S(2)}, u32[]{:S(2)}) %collective-permute-start.3) | collective-permute-done | bytes 229408 | tf_op jit(solution)/shard_map/ppermute | solution.py:281
  96.2 4.2 %collective-permute-done.10 = bf16[32,3584]{1,0:T(8,128)(2,1)S(1)} collective-permute-done((bf16[32,3584]{1,0:T(8,128)(2,1)S(1)}, bf16[32,3584]{1,0:T(8,128)(2,1)S(1)}, u32[]{:S(2)}, u32[]{:S(2)}) %collective-permute-start.10) | collective-permute-done | bytes 229408 | tf_op jit(solution)/shard_map/ppermute | solution.py:281
  104.6 2.3 %shard_map.97 = (bf16[64,3584]{1,0:T(8,128)(2,1)S(1)}, bf16[64,3584]{1,0:T(8,128)(2,1)S(1)}) custom-call(bf16[128,1024]{1,0:T(8,128)(2,1)S(1)} %multiply_convert_fusion.2.left_ref, bf16[1024,3584]{1,0:T(8,128)(2,1)S(1)} %get-tuple-element.34.right_ref), custom_call_target="tpu_custom_call" | custom-call | flops 939524096 | bytes 8519680 | tf_op jit(solution)/shard_map/pallas_call | solution.py:248
  107.0 12.7 %collective-permute-done.11 = bf16[128,1024]{1,0:T(8,128)(2,1)S(1)} collective-permute-done((bf16[128,1024]{1,0:T(8,128)(2,1)S(1)}, bf16[128,1024]{1,0:T(8,128)(2,1)S(1)}, u32[]{:S(2)}, u32[]{:S(2)}) %collective-permute-start.11) | collective-permute-done | bytes 262176 | tf_op jit(solution)/shard_map/ppermute | solution.py:300
  119.8 5.6 %collective-permute-done.12 = bf16[128,1024]{1,0:T(8,128)(2,1)S(1)} collective-permute-done((bf16[128,1024]{1,0:T(8,128)(2,1)S(1)}, bf16[128,1024]{1,0:T(8,128)(2,1)S(1)}, u32[]{:S(2)}, u32[]{:S(2)}) %collective-permute-start.12) | collective-permute-done | bytes 262176 | tf_op jit(solution)/shard_map/ppermute | solution.py:300
  125.6 2.3 %shard_map.100 = (bf16[64,3584]{1,0:T(8,128)(2,1)S(1)}, bf16[64,3584]{1,0:T(8,128)(2,1)S(1)}) custom-call(bf16[128,1024]{1,0:T(8,128)(2,1)S(1)} %multiply_convert_fusion.1.left_ref, bf16[1024,3584]{1,0:T(8,128)(2,1)S(1)} %get-tuple-element.34.right_ref), custom_call_target="tpu_custom_call" | custom-call | flops 939524096 | bytes 8519680 | tf_op jit(solution)/shard_map/pallas_call | solution.py:248
  131.5 5.6 %shard_map.105 = (bf16[64,3584]{1,0:T(8,128)(2,1)S(1)}, bf16[64,3584]{1,0:T(8,128)(2,1)S(1)}, bf16[64,3584]{1,0:T(8,128)(2,1)S(1)}, bf16[64,3584]{1,0:T(8,128)(2,1)S(1)}) custom-call(bf16[256,2048]{1,0:T(8,128)(2,1)S(1)} %pad_maximum_fusion.1.left_ref, bf16[3584,2048]{1,0:T(8,128)(2,1)S(1)} %get-tuple-element.33.right_ref), custom_call_target="tpu_custom_call" | custom-call | flops 3758096384 | bytes 17563648 | tf_op jit(solution)/shard_map/pallas_call | solution.py:248
  137.1 1.4 collective-permute-start.27
  139.4 9.1 %fusion = bf16[1,3584,2048]{2,1,0:T(8,128)(2,1)} fusion(bf16[256,3584]{1,0:T(8,128)(2,1)} %copy-done.3, bf16[256,1024]{1,0:T(8,128)(2,1)S(1)} %get-tuple-element.59, bf16[256,1024]{1,0:T(8,128)(2,1)S(1)} %get-tuple-element.58), kind=kOutput, calls=%fused_computation.1 | convolution fusion | flops 3767533568 | bytes 17563648 | tf_op jit(solution)/shard_map/dot_general | solution.py:407
  148.5 5.2 %fusion.1 = bf16[1,1024,3584]{2,1,0:T(8,128)(2,1)} fusion(bf16[256,3584]{1,0:T(8,128)(2,1)S(1)} %constant_dynamic-update-slice_fusion.left_ref, bf16[128,1024]{1,0:T(8,128)(2,1)S(1)} %multiply_convert_fusion.1.left_ref, bf16[128,1024]{1,0:T(8,128)(2,1)S(1)} %multiply_convert_fusion.2.left_ref), kind=kOutput, calls=%fused_computation.3 | convolution fusion | flops 1883766784 | bytes 9699328 | tf_op jit(solution)/shard_map/dot_general | solution.py:404
  155.6 1.8 collective-permute-done.14
  158.6 11.0 %collective-permute-done.15 = bf16[64,3584]{1,0:T(8,128)(2,1)} collective-permute-done((bf16[64,3584]{1,0:T(8,128)(2,1)S(1)}, bf16[64,3584]{1,0:T(8,128)(2,1)}, u32[]{:S(2)}, u32[]{:S(2)}) %collective-permute-start.15) | collective-permute-done | bytes 458784 | tf_op jit(solution)/shard_map/ppermute | solution.py:281
  170.7 1.6 collective-permute-start.16
  177.4 7.1 %collective-permute-done.17.refs_2_ = bf16[64,3584]{1,0:T(8,128)(2,1)S(1)} collective-permute-done((bf16[64,3584]{1,0:T(8,128)(2,1)S(1)}, bf16[64,3584]{1,0:T(8,128)(2,1)S(1)}, u32[]{:S(2)}, u32[]{:S(2)}) %collective-permute-start.17) | collective-permute-done | bytes 458784 | tf_op jit(solution)/shard_map/ppermute | solution.py:281
  184.5 10.3 %collective-permute-done.18.refs_3_ = bf16[64,3584]{1,0:T(8,128)(2,1)S(1)} collective-permute-done((bf16[64,3584]{1,0:T(8,128)(2,1)S(1)}, bf16[64,3584]{1,0:T(8,128)(2,1)S(1)}, u32[]{:S(2)}, u32[]{:S(2)}) %collective-permute-start.18) | collective-permute-done | bytes 458784 | tf_op jit(solution)/shard_map/ppermute | solution.py:281
  194.8 3.8 %shard_map.101 = bf16[256,3584]{1,0:T(8,128)(2,1)} custom-call(s32[1]{0:T(128)} %bitcast.own_ref, s32[8,256]{1,0:T(8,128)S(1)} %bitcast.14, f32[8,256]{1,0:T(8,128)S(1)} %bitcast.18, bf16[64,3584]{1,0:T(8,128)(2,1)S(1)} %pad_maximum_fusion.2.refs_0_, bf16[64,3584]{1,0:T(8,128)(2,1)S(1)} %collective-permute-done.16.refs_1_, ...), custom_call_target="tpu_custom_call" | custom-call | flops 1409286144 | bytes 3670016 | tf_op jit(solution)/shard_map/pallas_call | solution.py:150
  198.6 18.3 %collective-permute-done.32.refs_3_ = bf16[64,3584]{1,0:T(8,128)(2,1)S(1)} collective-permute-done((bf16[64,3584]{1,0:T(8,128)(2,1)S(1)}, bf16[64,3584]{1,0:T(8,128)(2,1)S(1)}, u32[]{:S(2)}, u32[]{:S(2)}) %collective-permute-start.32) | collective-permute-done | bytes 458784 | tf_op jit(solution)/shard_map/ppermute | solution.py:281
  216.9 2.9 %shard_map.106 = bf16[256,3584]{1,0:T(8,128)(2,1)} custom-call(s32[1]{0:T(128)} %bitcast.own_ref, s32[8,256]{1,0:T(8,128)S(1)} %bitcast.15, f32[8,256]{1,0:T(8,128)S(1)} %bitcast.19, bf16[64,3584]{1,0:T(8,128)(2,1)S(1)} %pad_maximum_fusion.9.refs_0_, bf16[64,3584]{1,0:T(8,128)(2,1)S(1)} %collective-permute-done.30.refs_1_, ...), custom_call_target="tpu_custom_call" | custom-call | flops 469762048 | bytes 3670016 | tf_op jit(solution)/shard_map/pallas_call | solution.py:150
  (131 shorter events, 33.8 us)
Async XLA Ops:
  3.7 33.5 %collective-permute-start = (bf16[64,3584]{1,0:T(8,128)(2,1)}, bf16[64,3584]{1,0:T(8,128)(2,1)S(1)}, u32[]{:S(2)}, u32[]{:S(2)}) collective-permute-start(bf16[64,3584]{1,0:T(8,128)(2,1)} %get-tuple-element.32), channel_id=1, source_target_pairs={{0,4},{1,5},{2,6},{3,7},{4,0},{5,1},{6,2},{7,3},{8,12},{9,13},{10,... | collective-permute-start | bytes 1376264 | tf_op jit(solution)/shard_map/ppermute | solution.py:281
  3.9 82.7 %collective-permute-start.6 = (bf16[64,3584]{1,0:T(8,128)(2,1)}, bf16[64,3584]{1,0:T(8,128)(2,1)S(1)}, u32[]{:S(2)}, u32[]{:S(2)}) collective-permute-start(bf16[64,3584]{1,0:T(8,128)(2,1)} %get-tuple-element.36), channel_id=1, source_target_pairs={{0,8},{1,9},{2,10},{3,11},{4,12},{5,13},{6,14},{7,15},{8,0},{9,1},... | collective-permute-start | bytes 1376264 | tf_op jit(solution)/shard_map/ppermute | solution.py:281
  6.2 39.6 %collective-permute-start.7 = (bf16[64,3584]{1,0:T(8,128)(2,1)}, bf16[64,3584]{1,0:T(8,128)(2,1)S(1)}, u32[]{:S(2)}, u32[]{:S(2)}) collective-permute-start(bf16[64,3584]{1,0:T(8,128)(2,1)} %get-tuple-element.37), channel_id=1, source_target_pairs={{0,12},{1,13},{2,14},{3,15},{4,8},{5,9},{6,10},{7,11},{8,4},{9,5},... | collective-permute-start | bytes 1376264 | tf_op jit(solution)/shard_map/ppermute | solution.py:281
  9.7 10.2 %collective-permute-start.19 = (bf16[64,3584]{1,0:T(8,128)(2,1)}, bf16[64,3584]{1,0:T(8,128)(2,1)S(1)}, u32[]{:S(2)}, u32[]{:S(2)}) collective-permute-start(bf16[64,3584]{1,0:T(8,128)(2,1)} %get-tuple-element.43), channel_id=1, source_target_pairs={{0,1},{1,0},{2,3},{3,2},{4,5},{5,4},{6,7},{7,6},{8,9},{9,8},{10,11... | collective-permute-start | bytes 1376264 | tf_op jit(solution)/shard_map/ppermute | solution.py:281
  11.2 12.2 %collective-permute-start.20 = (bf16[64,3584]{1,0:T(8,128)(2,1)}, bf16[64,3584]{1,0:T(8,128)(2,1)S(1)}, u32[]{:S(2)}, u32[]{:S(2)}) collective-permute-start(bf16[64,3584]{1,0:T(8,128)(2,1)} %get-tuple-element.44), channel_id=1, source_target_pairs={{0,2},{1,3},{2,0},{3,1},{4,6},{5,7},{6,4},{7,5},{8,10},{9,11},{10,... | collective-permute-start | bytes 1376264 | tf_op jit(solution)/shard_map/ppermute | solution.py:281
  19.9 13.6 %collective-permute-start.21 = (bf16[64,3584]{1,0:T(8,128)(2,1)S(1)}, bf16[64,3584]{1,0:T(8,128)(2,1)S(1)}, u32[]{:S(2)}, u32[]{:S(2)}) collective-permute-start(bf16[64,3584]{1,0:T(8,128)(2,1)S(1)} %copy-done.10), channel_id=1, source_target_pairs={{0,3},{1,2},{2,1},{3,0},{4,7},{5,6},{6,5},{7,4},{8,11},{9,10},{10,... | collective-permute-start | bytes 1376264 | tf_op jit(solution)/shard_map/ppermute | solution.py:281
  33.5 55.0 %collective-permute-start.22 = (bf16[64,3584]{1,0:T(8,128)(2,1)S(1)}, bf16[64,3584]{1,0:T(8,128)(2,1)S(1)}, u32[]{:S(2)}, u32[]{:S(2)}) collective-permute-start(bf16[64,3584]{1,0:T(8,128)(2,1)S(1)} %pad_maximum_fusion.6), channel_id=1, source_target_pairs={{0,4},{1,5},{2,6},{3,7},{4,0},{5,1},{6,2},{7,3},{8,12},{9,13},{10,... | collective-permute-start | bytes 1376264 | tf_op jit(solution)/shard_map/ppermute | solution.py:281
  35.0 54.6 %collective-permute-start.23 = (bf16[64,3584]{1,0:T(8,128)(2,1)S(1)}, bf16[64,3584]{1,0:T(8,128)(2,1)S(1)}, u32[]{:S(2)}, u32[]{:S(2)}) collective-permute-start(bf16[64,3584]{1,0:T(8,128)(2,1)S(1)} %pad_maximum_fusion.7), channel_id=1, source_target_pairs={{0,8},{1,9},{2,10},{3,11},{4,12},{5,13},{6,14},{7,15},{8,0},{9,1},... | collective-permute-start | bytes 1376264 | tf_op jit(solution)/shard_map/ppermute | solution.py:281
  37.3 53.6 %collective-permute-start.24 = (bf16[64,3584]{1,0:T(8,128)(2,1)S(1)}, bf16[64,3584]{1,0:T(8,128)(2,1)S(1)}, u32[]{:S(2)}, u32[]{:S(2)}) collective-permute-start(bf16[64,3584]{1,0:T(8,128)(2,1)S(1)} %pad_maximum_fusion.8), channel_id=1, source_target_pairs={{0,12},{1,13},{2,14},{3,15},{4,8},{5,9},{6,10},{7,11},{8,4},{9,5},... | collective-permute-start | bytes 1376264 | tf_op jit(solution)/shard_map/ppermute | solution.py:281
  45.9 23.9 %collective-permute-start.1 = (bf16[32,3584]{1,0:T(8,128)(2,1)S(1)}, bf16[32,3584]{1,0:T(8,128)(2,1)S(1)}, u32[]{:S(2)}, u32[]{:S(2)}) collective-permute-start(bf16[32,3584]{1,0:T(8,128)(2,1)S(1)} %pad_maximum_fusion.13), channel_id=1, source_target_pairs={{0,1},{1,0},{2,3},{3,2},{4,5},{5,4},{6,7},{7,6},{8,9},{9,8},{10,11... | collective-permute-start | bytes 688136 | tf_op jit(solution)/shard_map/ppermute | solution.py:281
  69.8 6.8 %collective-permute-start.2 = (bf16[32,3584]{1,0:T(8,128)(2,1)S(1)}, bf16[32,3584]{1,0:T(8,128)(2,1)S(1)}, u32[]{:S(2)}, u32[]{:S(2)}) collective-permute-start(bf16[32,3584]{1,0:T(8,128)(2,1)S(1)} %pad_maximum_fusion.14), channel_id=1, source_target_pairs={{0,2},{1,3},{2,0},{3,1},{4,6},{5,7},{6,4},{7,5},{8,10},{9,11},{10,... | collective-permute-start | bytes 688136 | tf_op jit(solution)/shard_map/ppermute | solution.py:281
  76.6 7.7 %collective-permute-start.3 = (bf16[32,3584]{1,0:T(8,128)(2,1)S(1)}, bf16[32,3584]{1,0:T(8,128)(2,1)S(1)}, u32[]{:S(2)}, u32[]{:S(2)}) collective-permute-start(bf16[32,3584]{1,0:T(8,128)(2,1)S(1)} %pad_maximum_fusion.15), channel_id=1, source_target_pairs={{0,3},{1,2},{2,1},{3,0},{4,7},{5,6},{6,5},{7,4},{8,11},{9,10},{10,... | collective-permute-start | bytes 688136 | tf_op jit(solution)/shard_map/ppermute | solution.py:281
  86.7 5.7 %collective-permute-start.8 = (bf16[32,3584]{1,0:T(8,128)(2,1)S(1)}, bf16[32,3584]{1,0:T(8,128)(2,1)S(1)}, u32[]{:S(2)}, u32[]{:S(2)}) collective-permute-start(bf16[32,3584]{1,0:T(8,128)(2,1)S(1)} %pad_maximum_fusion.16), channel_id=1, source_target_pairs={{0,1},{1,0},{2,3},{3,2},{4,5},{5,4},{6,7},{7,6},{8,9},{9,8},{10,11... | collective-permute-start | bytes 688136 | tf_op jit(solution)/shard_map/ppermute | solution.py:281
  87.7 7.2 %collective-permute-start.9 = (bf16[32,3584]{1,0:T(8,128)(2,1)S(1)}, bf16[32,3584]{1,0:T(8,128)(2,1)S(1)}, u32[]{:S(2)}, u32[]{:S(2)}) collective-permute-start(bf16[32,3584]{1,0:T(8,128)(2,1)S(1)} %pad_maximum_fusion.17), channel_id=1, source_target_pairs={{0,2},{1,3},{2,0},{3,1},{4,6},{5,7},{6,4},{7,5},{8,10},{9,11},{10,... | collective-permute-start | bytes 688136 | tf_op jit(solution)/shard_map/ppermute | solution.py:281
  88.5 11.8 %collective-permute-start.10 = (bf16[32,3584]{1,0:T(8,128)(2,1)S(1)}, bf16[32,3584]{1,0:T(8,128)(2,1)S(1)}, u32[]{:S(2)}, u32[]{:S(2)}) collective-permute-start(bf16[32,3584]{1,0:T(8,128)(2,1)S(1)} %pad_maximum_fusion.18), channel_id=1, source_target_pairs={{0,3},{1,2},{2,1},{3,0},{4,7},{5,6},{6,5},{7,4},{8,11},{9,10},{10,... | collective-permute-start | bytes 688136 | tf_op jit(solution)/shard_map/ppermute | solution.py:281
  89.6 14.4 %collective-permute-start.4 = (bf16[128,1024]{1,0:T(8,128)(2,1)S(1)}, bf16[128,1024]{1,0:T(8,128)(2,1)S(1)}, u32[]{:S(2)}, u32[]{:S(2)}) collective-permute-start(bf16[128,1024]{1,0:T(8,128)(2,1)S(1)} %shard_map.95), channel_id=1, source_target_pairs={{0,16},{16,0},{1,17},{17,1},{2,18},{18,2},{3,19},{19,3},{4,20},{20... | collective-permute-start | bytes 786440 | tf_op jit(solution)/shard_map/ppermute | solution.py:300
  90.9 13.5 %collective-permute-start.5 = (bf16[128,1024]{1,0:T(8,128)(2,1)S(1)}, bf16[128,1024]{1,0:T(8,128)(2,1)S(1)}, u32[]{:S(2)}, u32[]{:S(2)}) collective-permute-start(bf16[128,1024]{1,0:T(8,128)(2,1)S(1)} %shard_map.96), channel_id=1, source_target_pairs={{0,16},{16,0},{1,17},{17,1},{2,18},{18,2},{3,19},{19,3},{4,20},{20... | collective-permute-start | bytes 786440 | tf_op jit(solution)/shard_map/ppermute | solution.py:300
  92.4 38.1 %collective-permute-start.25 = (bf16[256,512]{1,0:T(8,128)(2,1)S(1)}, bf16[256,512]{1,0:T(8,128)(2,1)S(1)}, u32[]{:S(2)}, u32[]{:S(2)}) collective-permute-start(bf16[256,512]{1,0:T(8,128)(2,1)S(1)} %shard_map.103), channel_id=1, source_target_pairs={{0,16},{16,0},{1,17},{17,1},{2,18},{18,2},{3,19},{19,3},{4,20},{20... | collective-permute-start | bytes 786440 | tf_op jit(solution)/shard_map/ppermute | solution.py:300
  94.9 35.7 %collective-permute-start.26 = (bf16[256,512]{1,0:T(8,128)(2,1)S(1)}, bf16[256,512]{1,0:T(8,128)(2,1)S(1)}, u32[]{:S(2)}, u32[]{:S(2)}) collective-permute-start(bf16[256,512]{1,0:T(8,128)(2,1)S(1)} %shard_map.104), channel_id=1, source_target_pairs={{0,16},{16,0},{1,17},{17,1},{2,18},{18,2},{3,19},{19,3},{4,20},{20... | collective-permute-start | bytes 786440 | tf_op jit(solution)/shard_map/ppermute | solution.py:300
  101.7 18.1 %collective-permute-start.11 = (bf16[128,1024]{1,0:T(8,128)(2,1)S(1)}, bf16[128,1024]{1,0:T(8,128)(2,1)S(1)}, u32[]{:S(2)}, u32[]{:S(2)}) collective-permute-start(bf16[128,1024]{1,0:T(8,128)(2,1)S(1)} %shard_map.98), channel_id=1, source_target_pairs={{0,16},{16,0},{1,17},{17,1},{2,18},{18,2},{3,19},{19,3},{4,20},{20... | collective-permute-start | bytes 786440 | tf_op jit(solution)/shard_map/ppermute | solution.py:300
  104.0 21.4 %collective-permute-start.12 = (bf16[128,1024]{1,0:T(8,128)(2,1)S(1)}, bf16[128,1024]{1,0:T(8,128)(2,1)S(1)}, u32[]{:S(2)}, u32[]{:S(2)}) collective-permute-start(bf16[128,1024]{1,0:T(8,128)(2,1)S(1)} %shard_map.99), channel_id=1, source_target_pairs={{0,16},{16,0},{1,17},{17,1},{2,18},{18,2},{3,19},{19,3},{4,20},{20... | collective-permute-start | bytes 786440 | tf_op jit(solution)/shard_map/ppermute | solution.py:300
  106.9 46.7 %collective-permute-start.13 = (bf16[64,3584]{1,0:T(8,128)(2,1)S(1)}, bf16[64,3584]{1,0:T(8,128)(2,1)}, u32[]{:S(2)}, u32[]{:S(2)}) collective-permute-start(bf16[64,3584]{1,0:T(8,128)(2,1)S(1)} %get-tuple-element.39), channel_id=1, source_target_pairs={{0,4},{1,5},{2,6},{3,7},{4,0},{5,1},{6,2},{7,3},{8,12},{9,13},{10,... | collective-permute-start | bytes 1376264 | tf_op jit(solution)/shard_map/ppermute | solution.py:281
  128.7 28.8 %collective-permute-start.14 = (bf16[64,3584]{1,0:T(8,128)(2,1)S(1)}, bf16[64,3584]{1,0:T(8,128)(2,1)}, u32[]{:S(2)}, u32[]{:S(2)}) collective-permute-start(bf16[64,3584]{1,0:T(8,128)(2,1)S(1)} %get-tuple-element.40), channel_id=1, source_target_pairs={{0,8},{1,9},{2,10},{3,11},{4,12},{5,13},{6,14},{7,15},{8,0},{9,1},... | collective-permute-start | bytes 1376264 | tf_op jit(solution)/shard_map/ppermute | solution.py:281
  128.7 40.8 %collective-permute-start.15 = (bf16[64,3584]{1,0:T(8,128)(2,1)S(1)}, bf16[64,3584]{1,0:T(8,128)(2,1)}, u32[]{:S(2)}, u32[]{:S(2)}) collective-permute-start(bf16[64,3584]{1,0:T(8,128)(2,1)S(1)} %get-tuple-element.41), channel_id=1, source_target_pairs={{0,12},{1,13},{2,14},{3,15},{4,8},{5,9},{6,10},{7,11},{8,4},{9,5},... | collective-permute-start | bytes 1376264 | tf_op jit(solution)/shard_map/ppermute | solution.py:281
  137.1 36.4 %collective-permute-start.27 = (bf16[64,3584]{1,0:T(8,128)(2,1)S(1)}, bf16[64,3584]{1,0:T(8,128)(2,1)S(1)}, u32[]{:S(2)}, u32[]{:S(2)}) collective-permute-start(bf16[64,3584]{1,0:T(8,128)(2,1)S(1)} %get-tuple-element.55), channel_id=1, source_target_pairs={{0,1},{1,0},{2,3},{3,2},{4,5},{5,4},{6,7},{7,6},{8,9},{9,8},{10,11... | collective-permute-start | bytes 1376264 | tf_op jit(solution)/shard_map/ppermute | solution.py:281
  138.5 35.7 %collective-permute-start.28 = (bf16[64,3584]{1,0:T(8,128)(2,1)S(1)}, bf16[64,3584]{1,0:T(8,128)(2,1)S(1)}, u32[]{:S(2)}, u32[]{:S(2)}) collective-permute-start(bf16[64,3584]{1,0:T(8,128)(2,1)S(1)} %get-tuple-element.56), channel_id=1, source_target_pairs={{0,2},{1,3},{2,0},{3,1},{4,6},{5,7},{6,4},{7,5},{8,10},{9,11},{10,... | collective-permute-start | bytes 1376264 | tf_op jit(solution)/shard_map/ppermute | solution.py:281
  153.7 20.6 %collective-permute-start.29 = (bf16[64,3584]{1,0:T(8,128)(2,1)S(1)}, bf16[64,3584]{1,0:T(8,128)(2,1)S(1)}, u32[]{:S(2)}, u32[]{:S(2)}) collective-permute-start(bf16[64,3584]{1,0:T(8,128)(2,1)S(1)} %get-tuple-element.57), channel_id=1, source_target_pairs={{0,3},{1,2},{2,1},{3,0},{4,7},{5,6},{6,5},{7,4},{8,11},{9,10},{10,... | collective-permute-start | bytes 1376264 | tf_op jit(solution)/shard_map/ppermute | solution.py:281
  172.4 12.1 %collective-permute-start.17 = (bf16[64,3584]{1,0:T(8,128)(2,1)S(1)}, bf16[64,3584]{1,0:T(8,128)(2,1)S(1)}, u32[]{:S(2)}, u32[]{:S(2)}) collective-permute-start(bf16[64,3584]{1,0:T(8,128)(2,1)S(1)} %pad_maximum_fusion.4), channel_id=1, source_target_pairs={{0,2},{1,3},{2,0},{3,1},{4,6},{5,7},{6,4},{7,5},{8,10},{9,11},{10,... | collective-permute-start | bytes 1376264 | tf_op jit(solution)/shard_map/ppermute | solution.py:281
  173.5 21.3 %collective-permute-start.18 = (bf16[64,3584]{1,0:T(8,128)(2,1)S(1)}, bf16[64,3584]{1,0:T(8,128)(2,1)S(1)}, u32[]{:S(2)}, u32[]{:S(2)}) collective-permute-start(bf16[64,3584]{1,0:T(8,128)(2,1)S(1)} %pad_maximum_fusion.5), channel_id=1, source_target_pairs={{0,3},{1,2},{2,1},{3,0},{4,7},{5,6},{6,5},{7,4},{8,11},{9,10},{10,... | collective-permute-start | bytes 1376264 | tf_op jit(solution)/shard_map/ppermute | solution.py:281
  174.4 24.2 %collective-permute-start.30 = (bf16[64,3584]{1,0:T(8,128)(2,1)S(1)}, bf16[64,3584]{1,0:T(8,128)(2,1)S(1)}, u32[]{:S(2)}, u32[]{:S(2)}) collective-permute-start(bf16[64,3584]{1,0:T(8,128)(2,1)S(1)} %pad_maximum_fusion.10), channel_id=1, source_target_pairs={{0,4},{1,5},{2,6},{3,7},{4,0},{5,1},{6,2},{7,3},{8,12},{9,13},{10,... | collective-permute-start | bytes 1376264 | tf_op jit(solution)/shard_map/ppermute | solution.py:281
  174.5 24.0 %collective-permute-start.31 = (bf16[64,3584]{1,0:T(8,128)(2,1)S(1)}, bf16[64,3584]{1,0:T(8,128)(2,1)S(1)}, u32[]{:S(2)}, u32[]{:S(2)}) collective-permute-start(bf16[64,3584]{1,0:T(8,128)(2,1)S(1)} %pad_maximum_fusion.11), channel_id=1, source_target_pairs={{0,8},{1,9},{2,10},{3,11},{4,12},{5,13},{6,14},{7,15},{8,0},{9,1},... | collective-permute-start | bytes 1376264 | tf_op jit(solution)/shard_map/ppermute | solution.py:281
  176.0 40.9 %collective-permute-start.32 = (bf16[64,3584]{1,0:T(8,128)(2,1)S(1)}, bf16[64,3584]{1,0:T(8,128)(2,1)S(1)}, u32[]{:S(2)}, u32[]{:S(2)}) collective-permute-start(bf16[64,3584]{1,0:T(8,128)(2,1)S(1)} %pad_maximum_fusion.12), channel_id=1, source_target_pairs={{0,12},{1,13},{2,14},{3,15},{4,8},{5,9},{6,10},{7,11},{8,4},{9,5},... | collective-permute-start | bytes 1376264 | tf_op jit(solution)/shard_map/ppermute | solution.py:281
  (12 other events, 123.7 us)

commit v3 on v2

--- a/solution.py
+++ b/solution.py
@@ -398,8 +398,11 @@
         expert_rows, scaled_cot, inner_weight, outer_weight, outer, inner
     )
     grad_pieces = trade(grad_pieces, 1)
-    grad_pieces = regroup(grad_pieces, outer)
-    back_grad = trade(grad_pieces, inner)
+    runs = []
+    for part in (grad_pieces[: inner // 2], grad_pieces[inner // 2 :]):
+        part = regroup(part, outer)
+        runs.append(trade(part, inner))
+    back_grad = [run[k] for k in range(outer) for run in runs]
 
     output_grad = lax.dot_general(
         active, scaled_cot, contract_rows, preferred_element_type=jnp.float32

time: 222 us -> 224 us (level)
  starting transfers between devices: 53.4 us -> 60.7 us
  waiting for transfers between devices: 105 us -> 100 us
    ppermute x27 -> x30, starting transfers between devices: 47.8 us -> 55.1 us  [trade(): got[k] = lax.ppermute(pieces[k], 'expert', pairs)]
    ppermute x27 -> x30, waiting for transfers between devices: 86.8 us -> 81.8 us  [trade(): got[k] = lax.ppermute(pieces[k], 'expert', pairs)]
  transfers between devices with their start and end apart: 33 -> 36, of which waited for: 15 -> 17; matrix products, arithmetic and copies ran while one was open for 10% -> 10% of each run, Pallas kernels for 13% -> 13%
where the time goes in v3:
time: 224 us; the launch traced here: 222 us
  waiting for transfers between devices  100 us (45%)
  starting transfers between devices  60.7 us (27%)
  Pallas kernels  35.3 us (16%)
  matrix products  14.3 us (6%)
  local copies, waits for them, and re-layouts  7.97 us (4%)
  other arithmetic  2.37 us (1%)
    ppermute x30, waiting for transfers between devices, trade(): got[k] = lax.ppermute(pieces[k], 'expert', pairs)  81.8 us
    ppermute x30, starting transfers between devices, trade(): got[k] = lax.ppermute(pieces[k], 'expert', pairs)  55.1 us
    ppermute x6, waiting for transfers between devices, dp_swap(): return lax.ppermute(part, 'dp', [(0, 1), (1, 0)])  18.4 us
    pallas_call x3, Pallas kernels, held_product(): pl.pallas_call(functools.partial(held_kernel, right_dim, block, groups),...  10.2 us
    dot_general x1, matrix products, body(): lax.dot_general(jnp.concatenate(expert_rows), hidden_cot, contract_rows,...  9.12 us
    pallas_call x6, Pallas kernels, part_product(): pl.pallas_call(functools.partial(kernel, first), in_specs=[pl.BlockSpec(m...  6.77 us
    pallas_call x2, Pallas kernels, combine_rows(): pl.pallas_call(functools.partial(combine_kernel, weighted, expert_count,...  6.67 us
    pallas_call x2, Pallas kernels, gather_rows(): pl.pallas_call(functools.partial(gather_kernel, scaled, slot_count, outer...  6.33 us
  transfers between devices with their start and end apart: 36, of which 17 were waited for; matrix products, arithmetic and copies ran while one was open for 10% of the time, Pallas kernels for 13%

profile of v3, /device:TPU:13, one launch (start us, length us, event | category | flops | bytes accessed | tf_op | source)
XLA Modules:
  0.0 222.1 jit_solution(17215587649520113680)
XLA Ops:
  0.6 3.1 %shard_map.93 = (bf16[64,3584]{1,0:T(8,128)(2,1)}, bf16[64,3584]{1,0:T(8,128)(2,1)}, bf16[64,3584]{1,0:T(8,128)(2,1)}, bf16[64,3584]{1,0:T(8,128)(2,1)}) custom-call(s32[1]{0:T(128)} %bitcast.own_ref, s32[8,256]{1,0:T(8,128)} %bitcast.12, f32[8,256]{1,0:T(8,128)} %bitcast.16, bf16[256,3584]{1,0:T(8,128)(2,1)} %rows_ref.2), custom_call_target="tpu_custom_call" | custom-call | flops 469762048 | bytes 3670016 | tf_op jit(solution)/shard_map/pallas_call | solution.py:85
  3.9 2.3 %collective-permute-start.6 = (bf16[64,3584]{1,0:T(8,128)(2,1)}, bf16[64,3584]{1,0:T(8,128)(2,1)S(1)}, u32[]{:S(2)}, u32[]{:S(2)}) collective-permute-start(bf16[64,3584]{1,0:T(8,128)(2,1)} %get-tuple-element.36), channel_id=1, source_target_pairs={{0,8},{1,9},{2,10},{3,11},{4,12},{5,13},{6,14},{7,15},{8,0},{9,1},... | collective-permute-start | bytes 1376264 | tf_op jit(solution)/shard_map/ppermute | solution.py:281
  6.4 3.2 %shard_map.102 = (bf16[64,3584]{1,0:T(8,128)(2,1)}, bf16[64,3584]{1,0:T(8,128)(2,1)}, bf16[64,3584]{1,0:T(8,128)(2,1)}, bf16[64,3584]{1,0:T(8,128)(2,1)}) custom-call(s32[1]{0:T(128)} %bitcast.own_ref, s32[8,256]{1,0:T(8,128)} %bitcast.13, f32[8,256]{1,0:T(8,128)} %bitcast.17, bf16[256,3584]{1,0:T(8,128)(2,1)} %rows_ref.3), custom_call_target="tpu_custom_call" | custom-call | flops 469762048 | bytes 3670016 | tf_op jit(solution)/shard_map/pallas_call | solution.py:85
  11.4 3.1 %copy-done = bf16[1,1024,3584]{2,1,0:T(8,128)(2,1)S(1)} copy-done((bf16[1,1024,3584]{2,1,0:T(8,128)(2,1)S(1)}, bf16[1,1024,3584]{2,1,0:T(8,128)(2,1)}, u32[]{:S(2)}) %copy-start) | copy-done | bytes 7340056
  14.5 5.3 %shard_map.94 = (bf16[3584,2048]{1,0:T(8,128)(2,1)S(1)}, bf16[1024,3584]{1,0:T(8,128)(2,1)S(1)}) custom-call(bf16[3584,2048]{1,0:T(8,128)(2,1)} %bitcast.20, bf16[1024,3584]{1,0:T(8,128)(2,1)S(1)} %bitcast.11), custom_call_target="tpu_custom_call" | custom-call | bytes 44040192 | tf_op jit(solution)/shard_map/pallas_call | solution.py:194
  19.9 1.5 collective-permute-start.21
  21.4 1.9 collective-permute-done.20
  23.4 10.0 %collective-permute-done.21 = bf16[64,3584]{1,0:T(8,128)(2,1)S(1)} collective-permute-done((bf16[64,3584]{1,0:T(8,128)(2,1)S(1)}, bf16[64,3584]{1,0:T(8,128)(2,1)S(1)}, u32[]{:S(2)}, u32[]{:S(2)}) %collective-permute-start.21) | collective-permute-done | bytes 458784 | tf_op jit(solution)/shard_map/ppermute | solution.py:281
  35.0 2.2 %collective-permute-start.23 = (bf16[64,3584]{1,0:T(8,128)(2,1)S(1)}, bf16[64,3584]{1,0:T(8,128)(2,1)S(1)}, u32[]{:S(2)}, u32[]{:S(2)}) collective-permute-start(bf16[64,3584]{1,0:T(8,128)(2,1)S(1)} %pad_maximum_fusion.7), channel_id=1, source_target_pairs={{0,8},{1,9},{2,10},{3,11},{4,12},{5,13},{6,14},{7,15},{8,0},{9,1},... | collective-permute-start | bytes 1376264 | tf_op jit(solution)/shard_map/ppermute | solution.py:281
  37.7 8.2 %collective-permute-done.7 = bf16[64,3584]{1,0:T(8,128)(2,1)S(1)} collective-permute-done((bf16[64,3584]{1,0:T(8,128)(2,1)}, bf16[64,3584]{1,0:T(8,128)(2,1)S(1)}, u32[]{:S(2)}, u32[]{:S(2)}) %collective-permute-start.7) | collective-permute-done | bytes 458784 | tf_op jit(solution)/shard_map/ppermute | solution.py:281
  45.9 22.8 %collective-permute-start.1 = (bf16[32,3584]{1,0:T(8,128)(2,1)S(1)}, bf16[32,3584]{1,0:T(8,128)(2,1)S(1)}, u32[]{:S(2)}, u32[]{:S(2)}) collective-permute-start(bf16[32,3584]{1,0:T(8,128)(2,1)S(1)} %pad_maximum_fusion.9), channel_id=1, source_target_pairs={{0,1},{1,0},{2,3},{3,2},{4,5},{5,4},{6,7},{7,6},{8,9},{9,8},{10,11... | collective-permute-start | bytes 688136 | tf_op jit(solution)/shard_map/ppermute | solution.py:281
  70.0 6.5 %collective-permute-done.2 = bf16[32,3584]{1,0:T(8,128)(2,1)S(1)} collective-permute-done((bf16[32,3584]{1,0:T(8,128)(2,1)S(1)}, bf16[32,3584]{1,0:T(8,128)(2,1)S(1)}, u32[]{:S(2)}, u32[]{:S(2)}) %collective-permute-start.2) | collective-permute-done | bytes 229408 | tf_op jit(solution)/shard_map/ppermute | solution.py:281
  77.9 6.3 %collective-permute-done.3 = bf16[32,3584]{1,0:T(8,128)(2,1)S(1)} collective-permute-done((bf16[32,3584]{1,0:T(8,128)(2,1)S(1)}, bf16[32,3584]{1,0:T(8,128)(2,1)S(1)}, u32[]{:S(2)}, u32[]{:S(2)}) %collective-permute-start.3) | collective-permute-done | bytes 229408 | tf_op jit(solution)/shard_map/ppermute | solution.py:281
  96.2 4.2 %collective-permute-done.10 = bf16[32,3584]{1,0:T(8,128)(2,1)S(1)} collective-permute-done((bf16[32,3584]{1,0:T(8,128)(2,1)S(1)}, bf16[32,3584]{1,0:T(8,128)(2,1)S(1)}, u32[]{:S(2)}, u32[]{:S(2)}) %collective-permute-start.10) | collective-permute-done | bytes 229408 | tf_op jit(solution)/shard_map/ppermute | solution.py:281
  104.6 2.3 %shard_map.97 = (bf16[64,3584]{1,0:T(8,128)(2,1)S(1)}, bf16[64,3584]{1,0:T(8,128)(2,1)S(1)}) custom-call(bf16[128,1024]{1,0:T(8,128)(2,1)S(1)} %multiply_convert_fusion.2.left_ref, bf16[1024,3584]{1,0:T(8,128)(2,1)S(1)} %get-tuple-element.34.right_ref), custom_call_target="tpu_custom_call" | custom-call | flops 939524096 | bytes 8519680 | tf_op jit(solution)/shard_map/pallas_call | solution.py:248
  107.0 12.7 %collective-permute-done.11 = bf16[128,1024]{1,0:T(8,128)(2,1)S(1)} collective-permute-done((bf16[128,1024]{1,0:T(8,128)(2,1)S(1)}, bf16[128,1024]{1,0:T(8,128)(2,1)S(1)}, u32[]{:S(2)}, u32[]{:S(2)}) %collective-permute-start.11) | collective-permute-done | bytes 262176 | tf_op jit(solution)/shard_map/ppermute | solution.py:300
  119.8 5.6 %collective-permute-done.12 = bf16[128,1024]{1,0:T(8,128)(2,1)S(1)} collective-permute-done((bf16[128,1024]{1,0:T(8,128)(2,1)S(1)}, bf16[128,1024]{1,0:T(8,128)(2,1)S(1)}, u32[]{:S(2)}, u32[]{:S(2)}) %collective-permute-start.12) | collective-permute-done | bytes 262176 | tf_op jit(solution)/shard_map/ppermute | solution.py:300
  125.6 2.3 %shard_map.100 = (bf16[64,3584]{1,0:T(8,128)(2,1)S(1)}, bf16[64,3584]{1,0:T(8,128)(2,1)S(1)}) custom-call(bf16[128,1024]{1,0:T(8,128)(2,1)S(1)} %multiply_convert_fusion.1.left_ref, bf16[1024,3584]{1,0:T(8,128)(2,1)S(1)} %get-tuple-element.34.right_ref), custom_call_target="tpu_custom_call" | custom-call | flops 939524096 | bytes 8519680 | tf_op jit(solution)/shard_map/pallas_call | solution.py:248
  131.5 5.6 %shard_map.105 = (bf16[64,3584]{1,0:T(8,128)(2,1)S(1)}, bf16[64,3584]{1,0:T(8,128)(2,1)S(1)}, bf16[64,3584]{1,0:T(8,128)(2,1)S(1)}, bf16[64,3584]{1,0:T(8,128)(2,1)S(1)}) custom-call(bf16[256,2048]{1,0:T(8,128)(2,1)S(1)} %pad_maximum_fusion.1.left_ref, bf16[3584,2048]{1,0:T(8,128)(2,1)S(1)} %get-tuple-element.33.right_ref), custom_call_target="tpu_custom_call" | custom-call | flops 3758096384 | bytes 17563648 | tf_op jit(solution)/shard_map/pallas_call | solution.py:248
  139.4 9.1 %fusion = bf16[1,3584,2048]{2,1,0:T(8,128)(2,1)} fusion(bf16[256,3584]{1,0:T(8,128)(2,1)} %copy-done.3, bf16[256,1024]{1,0:T(8,128)(2,1)S(1)} %get-tuple-element.59, bf16[256,1024]{1,0:T(8,128)(2,1)S(1)} %get-tuple-element.58), kind=kOutput, calls=%fused_computation.1 | convolution fusion | flops 3767533568 | bytes 17563648 | tf_op jit(solution)/shard_map/dot_general | solution.py:410
  148.5 5.2 %fusion.1 = bf16[1,1024,3584]{2,1,0:T(8,128)(2,1)} fusion(bf16[256,3584]{1,0:T(8,128)(2,1)S(1)} %constant_dynamic-update-slice_fusion.left_ref, bf16[128,1024]{1,0:T(8,128)(2,1)S(1)} %multiply_convert_fusion.1.left_ref, bf16[128,1024]{1,0:T(8,128)(2,1)S(1)} %multiply_convert_fusion.2.left_ref), kind=kOutput, calls=%fused_computation.3 | convolution fusion | flops 1883766784 | bytes 9699328 | tf_op jit(solution)/shard_map/dot_general | solution.py:407
  155.6 1.9 collective-permute-done.14
  158.6 11.0 %collective-permute-done.15 = bf16[64,3584]{1,0:T(8,128)(2,1)} collective-permute-done((bf16[64,3584]{1,0:T(8,128)(2,1)S(1)}, bf16[64,3584]{1,0:T(8,128)(2,1)}, u32[]{:S(2)}, u32[]{:S(2)}) %collective-permute-start.15) | collective-permute-done | bytes 458784 | tf_op jit(solution)/shard_map/ppermute | solution.py:281
  170.7 1.6 collective-permute-start.16
  176.6 4.6 %collective-permute-done.30.refs_2_ = bf16[32,3584]{1,0:T(8,128)(2,1)S(1)} collective-permute-done((bf16[32,3584]{1,0:T(8,128)(2,1)S(1)}, bf16[32,3584]{1,0:T(8,128)(2,1)S(1)}, u32[]{:S(2)}, u32[]{:S(2)}) %collective-permute-start.30) | collective-permute-done | bytes 229408 | tf_op jit(solution)/shard_map/ppermute | solution.py:281
  182.3 2.1 collective-permute-done.32.refs_4_
  184.4 6.7 %collective-permute-start.18 = (bf16[64,3584]{1,0:T(8,128)(2,1)S(1)}, bf16[64,3584]{1,0:T(8,128)(2,1)S(1)}, u32[]{:S(2)}, u32[]{:S(2)}) collective-permute-start(bf16[64,3584]{1,0:T(8,128)(2,1)S(1)} %pad_maximum_fusion.5), channel_id=1, source_target_pairs={{0,3},{1,2},{2,1},{3,0},{4,7},{5,6},{6,5},{7,4},{8,11},{9,10},{10,... | collective-permute-start | bytes 1376264 | tf_op jit(solution)/shard_map/ppermute | solution.py:281
  191.1 4.2 %collective-permute-done.34.refs_6_ = bf16[32,3584]{1,0:T(8,128)(2,1)S(1)} collective-permute-done((bf16[32,3584]{1,0:T(8,128)(2,1)S(1)}, bf16[32,3584]{1,0:T(8,128)(2,1)S(1)}, u32[]{:S(2)}, u32[]{:S(2)}) %collective-permute-start.34) | collective-permute-done | bytes 229408 | tf_op jit(solution)/shard_map/ppermute | solution.py:281
  195.7 13.8 %collective-permute-done.33.refs_5_ = bf16[32,3584]{1,0:T(8,128)(2,1)S(1)} collective-permute-done((bf16[32,3584]{1,0:T(8,128)(2,1)S(1)}, bf16[32,3584]{1,0:T(8,128)(2,1)S(1)}, u32[]{:S(2)}, u32[]{:S(2)}) %collective-permute-start.33) | collective-permute-done | bytes 229408 | tf_op jit(solution)/shard_map/ppermute | solution.py:281
  209.5 5.9 %collective-permute-done.35.refs_7_ = bf16[32,3584]{1,0:T(8,128)(2,1)S(1)} collective-permute-done((bf16[32,3584]{1,0:T(8,128)(2,1)S(1)}, bf16[32,3584]{1,0:T(8,128)(2,1)S(1)}, u32[]{:S(2)}, u32[]{:S(2)}) %collective-permute-start.35) | collective-permute-done | bytes 229408 | tf_op jit(solution)/shard_map/ppermute | solution.py:281
  215.4 2.9 %shard_map.106 = bf16[256,3584]{1,0:T(8,128)(2,1)} custom-call(s32[1]{0:T(128)} %bitcast.own_ref, s32[8,256]{1,0:T(8,128)S(1)} %bitcast.14, f32[8,256]{1,0:T(8,128)S(1)} %bitcast.18, bf16[32,3584]{1,0:T(8,128)(2,1)S(1)} %pad_maximum_fusion.15.refs_0_, bf16[32,3584]{1,0:T(8,128)(2,1)S(1)} %pad_maximum_fusion.16.refs_1_, ...), custom_call_target="tpu_custom_call" | custom-call | flops 469762048 | bytes 3670016 | tf_op jit(solution)/shard_map/pallas_call | solution.py:150
  218.3 3.8 %shard_map.101 = bf16[256,3584]{1,0:T(8,128)(2,1)} custom-call(s32[1]{0:T(128)} %bitcast.own_ref, s32[8,256]{1,0:T(8,128)S(1)} %bitcast.15, f32[8,256]{1,0:T(8,128)S(1)} %bitcast.19, bf16[64,3584]{1,0:T(8,128)(2,1)S(1)} %pad_maximum_fusion.2.refs_0_, bf16[64,3584]{1,0:T(8,128)(2,1)S(1)} %collective-permute-done.16.refs_1_, ...), custom_call_target="tpu_custom_call" | custom-call | flops 1409286144 | bytes 3670016 | tf_op jit(solution)/shard_map/pallas_call | solution.py:150
  (141 shorter events, 38.7 us)
Async XLA Ops:
  3.7 33.5 %collective-permute-start = (bf16[64,3584]{1,0:T(8,128)(2,1)}, bf16[64,3584]{1,0:T(8,128)(2,1)S(1)}, u32[]{:S(2)}, u32[]{:S(2)}) collective-permute-start(bf16[64,3584]{1,0:T(8,128)(2,1)} %get-tuple-element.32), channel_id=1, source_target_pairs={{0,4},{1,5},{2,6},{3,7},{4,0},{5,1},{6,2},{7,3},{8,12},{9,13},{10,... | collective-permute-start | bytes 1376264 | tf_op jit(solution)/shard_map/ppermute | solution.py:281
  3.9 82.7 %collective-permute-start.6 = (bf16[64,3584]{1,0:T(8,128)(2,1)}, bf16[64,3584]{1,0:T(8,128)(2,1)S(1)}, u32[]{:S(2)}, u32[]{:S(2)}) collective-permute-start(bf16[64,3584]{1,0:T(8,128)(2,1)} %get-tuple-element.36), channel_id=1, source_target_pairs={{0,8},{1,9},{2,10},{3,11},{4,12},{5,13},{6,14},{7,15},{8,0},{9,1},... | collective-permute-start | bytes 1376264 | tf_op jit(solution)/shard_map/ppermute | solution.py:281
  6.2 39.6 %collective-permute-start.7 = (bf16[64,3584]{1,0:T(8,128)(2,1)}, bf16[64,3584]{1,0:T(8,128)(2,1)S(1)}, u32[]{:S(2)}, u32[]{:S(2)}) collective-permute-start(bf16[64,3584]{1,0:T(8,128)(2,1)} %get-tuple-element.37), channel_id=1, source_target_pairs={{0,12},{1,13},{2,14},{3,15},{4,8},{5,9},{6,10},{7,11},{8,4},{9,5},... | collective-permute-start | bytes 1376264 | tf_op jit(solution)/shard_map/ppermute | solution.py:281
  9.6 10.2 %collective-permute-start.19 = (bf16[64,3584]{1,0:T(8,128)(2,1)}, bf16[64,3584]{1,0:T(8,128)(2,1)S(1)}, u32[]{:S(2)}, u32[]{:S(2)}) collective-permute-start(bf16[64,3584]{1,0:T(8,128)(2,1)} %get-tuple-element.43), channel_id=1, source_target_pairs={{0,1},{1,0},{2,3},{3,2},{4,5},{5,4},{6,7},{7,6},{8,9},{9,8},{10,11... | collective-permute-start | bytes 1376264 | tf_op jit(solution)/shard_map/ppermute | solution.py:281
  11.2 12.2 %collective-permute-start.20 = (bf16[64,3584]{1,0:T(8,128)(2,1)}, bf16[64,3584]{1,0:T(8,128)(2,1)S(1)}, u32[]{:S(2)}, u32[]{:S(2)}) collective-permute-start(bf16[64,3584]{1,0:T(8,128)(2,1)} %get-tuple-element.44), channel_id=1, source_target_pairs={{0,2},{1,3},{2,0},{3,1},{4,6},{5,7},{6,4},{7,5},{8,10},{9,11},{10,... | collective-permute-start | bytes 1376264 | tf_op jit(solution)/shard_map/ppermute | solution.py:281
  19.9 13.6 %collective-permute-start.21 = (bf16[64,3584]{1,0:T(8,128)(2,1)S(1)}, bf16[64,3584]{1,0:T(8,128)(2,1)S(1)}, u32[]{:S(2)}, u32[]{:S(2)}) collective-permute-start(bf16[64,3584]{1,0:T(8,128)(2,1)S(1)} %copy-done.10), channel_id=1, source_target_pairs={{0,3},{1,2},{2,1},{3,0},{4,7},{5,6},{6,5},{7,4},{8,11},{9,10},{10,... | collective-permute-start | bytes 1376264 | tf_op jit(solution)/shard_map/ppermute | solution.py:281
  33.5 55.0 %collective-permute-start.22 = (bf16[64,3584]{1,0:T(8,128)(2,1)S(1)}, bf16[64,3584]{1,0:T(8,128)(2,1)S(1)}, u32[]{:S(2)}, u32[]{:S(2)}) collective-permute-start(bf16[64,3584]{1,0:T(8,128)(2,1)S(1)} %pad_maximum_fusion.6), channel_id=1, source_target_pairs={{0,4},{1,5},{2,6},{3,7},{4,0},{5,1},{6,2},{7,3},{8,12},{9,13},{10,... | collective-permute-start | bytes 1376264 | tf_op jit(solution)/shard_map/ppermute | solution.py:281
  35.0 54.6 %collective-permute-start.23 = (bf16[64,3584]{1,0:T(8,128)(2,1)S(1)}, bf16[64,3584]{1,0:T(8,128)(2,1)S(1)}, u32[]{:S(2)}, u32[]{:S(2)}) collective-permute-start(bf16[64,3584]{1,0:T(8,128)(2,1)S(1)} %pad_maximum_fusion.7), channel_id=1, source_target_pairs={{0,8},{1,9},{2,10},{3,11},{4,12},{5,13},{6,14},{7,15},{8,0},{9,1},... | collective-permute-start | bytes 1376264 | tf_op jit(solution)/shard_map/ppermute | solution.py:281
  37.2 53.6 %collective-permute-start.24 = (bf16[64,3584]{1,0:T(8,128)(2,1)S(1)}, bf16[64,3584]{1,0:T(8,128)(2,1)S(1)}, u32[]{:S(2)}, u32[]{:S(2)}) collective-permute-start(bf16[64,3584]{1,0:T(8,128)(2,1)S(1)} %pad_maximum_fusion.8), channel_id=1, source_target_pairs={{0,12},{1,13},{2,14},{3,15},{4,8},{5,9},{6,10},{7,11},{8,4},{9,5},... | collective-permute-start | bytes 1376264 | tf_op jit(solution)/shard_map/ppermute | solution.py:281
  45.9 23.9 %collective-permute-start.1 = (bf16[32,3584]{1,0:T(8,128)(2,1)S(1)}, bf16[32,3584]{1,0:T(8,128)(2,1)S(1)}, u32[]{:S(2)}, u32[]{:S(2)}) collective-permute-start(bf16[32,3584]{1,0:T(8,128)(2,1)S(1)} %pad_maximum_fusion.9), channel_id=1, source_target_pairs={{0,1},{1,0},{2,3},{3,2},{4,5},{5,4},{6,7},{7,6},{8,9},{9,8},{10,11... | collective-permute-start | bytes 688136 | tf_op jit(solution)/shard_map/ppermute | solution.py:281
  88.5 11.8 %collective-permute-start.10 = (bf16[32,3584]{1,0:T(8,128)(2,1)S(1)}, bf16[32,3584]{1,0:T(8,128)(2,1)S(1)}, u32[]{:S(2)}, u32[]{:S(2)}) collective-permute-start(bf16[32,3584]{1,0:T(8,128)(2,1)S(1)} %pad_maximum_fusion.14), channel_id=1, source_target_pairs={{0,3},{1,2},{2,1},{3,0},{4,7},{5,6},{6,5},{7,4},{8,11},{9,10},{10,... | collective-permute-start | bytes 688136 | tf_op jit(solution)/shard_map/ppermute | solution.py:281
  89.6 14.4 %collective-permute-start.4 = (bf16[128,1024]{1,0:T(8,128)(2,1)S(1)}, bf16[128,1024]{1,0:T(8,128)(2,1)S(1)}, u32[]{:S(2)}, u32[]{:S(2)}) collective-permute-start(bf16[128,1024]{1,0:T(8,128)(2,1)S(1)} %shard_map.95), channel_id=1, source_target_pairs={{0,16},{16,0},{1,17},{17,1},{2,18},{18,2},{3,19},{19,3},{4,20},{20... | collective-permute-start | bytes 786440 | tf_op jit(solution)/shard_map/ppermute | solution.py:300
  90.9 13.5 %collective-permute-start.5 = (bf16[128,1024]{1,0:T(8,128)(2,1)S(1)}, bf16[128,1024]{1,0:T(8,128)(2,1)S(1)}, u32[]{:S(2)}, u32[]{:S(2)}) collective-permute-start(bf16[128,1024]{1,0:T(8,128)(2,1)S(1)} %shard_map.96), channel_id=1, source_target_pairs={{0,16},{16,0},{1,17},{17,1},{2,18},{18,2},{3,19},{19,3},{4,20},{20... | collective-permute-start | bytes 786440 | tf_op jit(solution)/shard_map/ppermute | solution.py:300
  92.4 38.1 %collective-permute-start.25 = (bf16[256,512]{1,0:T(8,128)(2,1)S(1)}, bf16[256,512]{1,0:T(8,128)(2,1)S(1)}, u32[]{:S(2)}, u32[]{:S(2)}) collective-permute-start(bf16[256,512]{1,0:T(8,128)(2,1)S(1)} %shard_map.103), channel_id=1, source_target_pairs={{0,16},{16,0},{1,17},{17,1},{2,18},{18,2},{3,19},{19,3},{4,20},{20... | collective-permute-start | bytes 786440 | tf_op jit(solution)/shard_map/ppermute | solution.py:300
  94.9 35.7 %collective-permute-start.26 = (bf16[256,512]{1,0:T(8,128)(2,1)S(1)}, bf16[256,512]{1,0:T(8,128)(2,1)S(1)}, u32[]{:S(2)}, u32[]{:S(2)}) collective-permute-start(bf16[256,512]{1,0:T(8,128)(2,1)S(1)} %shard_map.104), channel_id=1, source_target_pairs={{0,16},{16,0},{1,17},{17,1},{2,18},{18,2},{3,19},{19,3},{4,20},{20... | collective-permute-start | bytes 786440 | tf_op jit(solution)/shard_map/ppermute | solution.py:300
  101.7 18.1 %collective-permute-start.11 = (bf16[128,1024]{1,0:T(8,128)(2,1)S(1)}, bf16[128,1024]{1,0:T(8,128)(2,1)S(1)}, u32[]{:S(2)}, u32[]{:S(2)}) collective-permute-start(bf16[128,1024]{1,0:T(8,128)(2,1)S(1)} %shard_map.98), channel_id=1, source_target_pairs={{0,16},{16,0},{1,17},{17,1},{2,18},{18,2},{3,19},{19,3},{4,20},{20... | collective-permute-start | bytes 786440 | tf_op jit(solution)/shard_map/ppermute | solution.py:300
  104.0 21.4 %collective-permute-start.12 = (bf16[128,1024]{1,0:T(8,128)(2,1)S(1)}, bf16[128,1024]{1,0:T(8,128)(2,1)S(1)}, u32[]{:S(2)}, u32[]{:S(2)}) collective-permute-start(bf16[128,1024]{1,0:T(8,128)(2,1)S(1)} %shard_map.99), channel_id=1, source_target_pairs={{0,16},{16,0},{1,17},{17,1},{2,18},{18,2},{3,19},{19,3},{4,20},{20... | collective-permute-start | bytes 786440 | tf_op jit(solution)/shard_map/ppermute | solution.py:300
  106.9 46.7 %collective-permute-start.13 = (bf16[64,3584]{1,0:T(8,128)(2,1)S(1)}, bf16[64,3584]{1,0:T(8,128)(2,1)}, u32[]{:S(2)}, u32[]{:S(2)}) collective-permute-start(bf16[64,3584]{1,0:T(8,128)(2,1)S(1)} %get-tuple-element.39), channel_id=1, source_target_pairs={{0,4},{1,5},{2,6},{3,7},{4,0},{5,1},{6,2},{7,3},{8,12},{9,13},{10,... | collective-permute-start | bytes 1376264 | tf_op jit(solution)/shard_map/ppermute | solution.py:281
  128.7 28.8 %collective-permute-start.14 = (bf16[64,3584]{1,0:T(8,128)(2,1)S(1)}, bf16[64,3584]{1,0:T(8,128)(2,1)}, u32[]{:S(2)}, u32[]{:S(2)}) collective-permute-start(bf16[64,3584]{1,0:T(8,128)(2,1)S(1)} %get-tuple-element.40), channel_id=1, source_target_pairs={{0,8},{1,9},{2,10},{3,11},{4,12},{5,13},{6,14},{7,15},{8,0},{9,1},... | collective-permute-start | bytes 1376264 | tf_op jit(solution)/shard_map/ppermute | solution.py:281
  128.7 40.8 %collective-permute-start.15 = (bf16[64,3584]{1,0:T(8,128)(2,1)S(1)}, bf16[64,3584]{1,0:T(8,128)(2,1)}, u32[]{:S(2)}, u32[]{:S(2)}) collective-permute-start(bf16[64,3584]{1,0:T(8,128)(2,1)S(1)} %get-tuple-element.41), channel_id=1, source_target_pairs={{0,12},{1,13},{2,14},{3,15},{4,8},{5,9},{6,10},{7,11},{8,4},{9,5},... | collective-permute-start | bytes 1376264 | tf_op jit(solution)/shard_map/ppermute | solution.py:281
  137.1 35.2 %collective-permute-start.27 = (bf16[64,3584]{1,0:T(8,128)(2,1)S(1)}, bf16[64,3584]{1,0:T(8,128)(2,1)S(1)}, u32[]{:S(2)}, u32[]{:S(2)}) collective-permute-start(bf16[64,3584]{1,0:T(8,128)(2,1)S(1)} %get-tuple-element.55), channel_id=1, source_target_pairs={{0,1},{1,0},{2,3},{3,2},{4,5},{5,4},{6,7},{7,6},{8,9},{9,8},{10,11... | collective-permute-start | bytes 1376264 | tf_op jit(solution)/shard_map/ppermute | solution.py:281
  138.5 35.4 %collective-permute-start.28 = (bf16[64,3584]{1,0:T(8,128)(2,1)S(1)}, bf16[64,3584]{1,0:T(8,128)(2,1)S(1)}, u32[]{:S(2)}, u32[]{:S(2)}) collective-permute-start(bf16[64,3584]{1,0:T(8,128)(2,1)S(1)} %get-tuple-element.56), channel_id=1, source_target_pairs={{0,2},{1,3},{2,0},{3,1},{4,6},{5,7},{6,4},{7,5},{8,10},{9,11},{10,... | collective-permute-start | bytes 1376264 | tf_op jit(solution)/shard_map/ppermute | solution.py:281
  153.7 21.7 %collective-permute-start.29 = (bf16[64,3584]{1,0:T(8,128)(2,1)S(1)}, bf16[64,3584]{1,0:T(8,128)(2,1)S(1)}, u32[]{:S(2)}, u32[]{:S(2)}) collective-permute-start(bf16[64,3584]{1,0:T(8,128)(2,1)S(1)} %get-tuple-element.57), channel_id=1, source_target_pairs={{0,3},{1,2},{2,1},{3,0},{4,7},{5,6},{6,5},{7,4},{8,11},{9,10},{10,... | collective-permute-start | bytes 1376264 | tf_op jit(solution)/shard_map/ppermute | solution.py:281
  170.7 47.6 %collective-permute-start.16 = (bf16[64,3584]{1,0:T(8,128)(2,1)S(1)}, bf16[64,3584]{1,0:T(8,128)(2,1)S(1)}, u32[]{:S(2)}, u32[]{:S(2)}) collective-permute-start(bf16[64,3584]{1,0:T(8,128)(2,1)S(1)} %pad_maximum_fusion.3), channel_id=1, source_target_pairs={{0,1},{1,0},{2,3},{3,2},{4,5},{5,4},{6,7},{7,6},{8,9},{9,8},{10,11... | collective-permute-start | bytes 1376264 | tf_op jit(solution)/shard_map/ppermute | solution.py:281
  172.4 8.9 %collective-permute-start.30 = (bf16[32,3584]{1,0:T(8,128)(2,1)S(1)}, bf16[32,3584]{1,0:T(8,128)(2,1)S(1)}, u32[]{:S(2)}, u32[]{:S(2)}) collective-permute-start(bf16[32,3584]{1,0:T(8,128)(2,1)S(1)} %pad_maximum_fusion.17), channel_id=1, source_target_pairs={{0,4},{1,5},{2,6},{3,7},{4,0},{5,1},{6,2},{7,3},{8,12},{9,13},{10,... | collective-permute-start | bytes 688136 | tf_op jit(solution)/shard_map/ppermute | solution.py:281
  172.5 11.9 %collective-permute-start.32 = (bf16[32,3584]{1,0:T(8,128)(2,1)S(1)}, bf16[32,3584]{1,0:T(8,128)(2,1)S(1)}, u32[]{:S(2)}, u32[]{:S(2)}) collective-permute-start(bf16[32,3584]{1,0:T(8,128)(2,1)S(1)} %pad_maximum_fusion.19), channel_id=1, source_target_pairs={{0,8},{1,9},{2,10},{3,11},{4,12},{5,13},{6,14},{7,15},{8,0},{9,1},... | collective-permute-start | bytes 688136 | tf_op jit(solution)/shard_map/ppermute | solution.py:281
  173.9 21.5 %collective-permute-start.34 = (bf16[32,3584]{1,0:T(8,128)(2,1)S(1)}, bf16[32,3584]{1,0:T(8,128)(2,1)S(1)}, u32[]{:S(2)}, u32[]{:S(2)}) collective-permute-start(bf16[32,3584]{1,0:T(8,128)(2,1)S(1)} %pad_maximum_fusion.21), channel_id=1, source_target_pairs={{0,12},{1,13},{2,14},{3,15},{4,8},{5,9},{6,10},{7,11},{8,4},{9,5},... | collective-permute-start | bytes 688136 | tf_op jit(solution)/shard_map/ppermute | solution.py:281
  175.4 20.0 %collective-permute-start.31 = (bf16[32,3584]{1,0:T(8,128)(2,1)S(1)}, bf16[32,3584]{1,0:T(8,128)(2,1)S(1)}, u32[]{:S(2)}, u32[]{:S(2)}) collective-permute-start(bf16[32,3584]{1,0:T(8,128)(2,1)S(1)} %pad_maximum_fusion.18), channel_id=1, source_target_pairs={{0,4},{1,5},{2,6},{3,7},{4,0},{5,1},{6,2},{7,3},{8,12},{9,13},{10,... | collective-permute-start | bytes 688136 | tf_op jit(solution)/shard_map/ppermute | solution.py:281
  181.2 37.0 %collective-permute-start.17 = (bf16[64,3584]{1,0:T(8,128)(2,1)S(1)}, bf16[64,3584]{1,0:T(8,128)(2,1)S(1)}, u32[]{:S(2)}, u32[]{:S(2)}) collective-permute-start(bf16[64,3584]{1,0:T(8,128)(2,1)S(1)} %pad_maximum_fusion.4), channel_id=1, source_target_pairs={{0,2},{1,3},{2,0},{3,1},{4,6},{5,7},{6,4},{7,5},{8,10},{9,11},{10,... | collective-permute-start | bytes 1376264 | tf_op jit(solution)/shard_map/ppermute | solution.py:281
  184.4 33.9 %collective-permute-start.18 = (bf16[64,3584]{1,0:T(8,128)(2,1)S(1)}, bf16[64,3584]{1,0:T(8,128)(2,1)S(1)}, u32[]{:S(2)}, u32[]{:S(2)}) collective-permute-start(bf16[64,3584]{1,0:T(8,128)(2,1)S(1)} %pad_maximum_fusion.5), channel_id=1, source_target_pairs={{0,3},{1,2},{2,1},{3,0},{4,7},{5,6},{6,5},{7,4},{8,11},{9,10},{10,... | collective-permute-start | bytes 1376264 | tf_op jit(solution)/shard_map/ppermute | solution.py:281
  195.4 14.1 %collective-permute-start.33 = (bf16[32,3584]{1,0:T(8,128)(2,1)S(1)}, bf16[32,3584]{1,0:T(8,128)(2,1)S(1)}, u32[]{:S(2)}, u32[]{:S(2)}) collective-permute-start(bf16[32,3584]{1,0:T(8,128)(2,1)S(1)} %pad_maximum_fusion.20), channel_id=1, source_target_pairs={{0,8},{1,9},{2,10},{3,11},{4,12},{5,13},{6,14},{7,15},{8,0},{9,1},... | collective-permute-start | bytes 688136 | tf_op jit(solution)/shard_map/ppermute | solution.py:281
  195.4 20.0 %collective-permute-start.35 = (bf16[32,3584]{1,0:T(8,128)(2,1)S(1)}, bf16[32,3584]{1,0:T(8,128)(2,1)S(1)}, u32[]{:S(2)}, u32[]{:S(2)}) collective-permute-start(bf16[32,3584]{1,0:T(8,128)(2,1)S(1)} %pad_maximum_fusion.22), channel_id=1, source_target_pairs={{0,12},{1,13},{2,14},{3,15},{4,8},{5,9},{6,10},{7,11},{8,4},{9,5},... | collective-permute-start | bytes 688136 | tf_op jit(solution)/shard_map/ppermute | solution.py:281
  (15 other events, 149.7 us)

commit v4 on v3

--- a/solution.py
+++ b/solution.py
@@ -48,7 +48,7 @@
 
 def gather_kernel(scaled, slot_count, outer, held, own_ref, route_ref, gate_ref, rows_ref, *refs):
     refs = refs[held:]
-    out_refs, (placed_ref, gain_ref) = refs[:-2], refs[-2:]
+    out_refs, (table_ref, placed_ref, gain_ref) = refs[:-3], refs[-3:]
     row_total, tok_count = placed_ref.shape
     expert_count, piece_rows = row_total // slot_count, out_refs[0].shape[0]
 
@@ -67,6 +67,7 @@
                 gain_ref[here, :] = jnp.sum(
                     jnp.where(matched, gates[e : e + 1, :], 0.0), axis=1, keepdims=True
                 )
+        table_ref[...] = placed_ref[...]
 
     picked = jnp.dot(placed_ref[...], rows_ref[...], preferred_element_type=jnp.float32)
     if scaled:
@@ -92,8 +93,10 @@
             pl.BlockSpec((tok_count, block), lambda i: (0, i)),
         ]
         + [pl.BlockSpec(memory_space=pl.ANY)] * len(held),
-        out_specs=[pl.BlockSpec((piece_rows, block), lambda i: (0, i))] * pieces,
-        out_shape=[jax.ShapeDtypeStruct((piece_rows, width), jnp.bfloat16)] * pieces,
+        out_specs=[pl.BlockSpec((piece_rows, block), lambda i: (0, i))] * pieces
+        + [pl.BlockSpec((row_total, tok_count), lambda i: (0, 0))],
+        out_shape=[jax.ShapeDtypeStruct((piece_rows, width), jnp.bfloat16)] * pieces
+        + [jax.ShapeDtypeStruct((row_total, tok_count), jnp.bfloat16)],
         scratch_shapes=[
             pltpu.VMEM((row_total, tok_count), jnp.bfloat16),
             pltpu.VMEM((row_total, 1), jnp.float32),
@@ -144,7 +147,7 @@
 def combine_rows(own, routes, gates, pieces, expert_count, weighted, outer):
     tok_count = routes.shape[1]
     row_total, width = sum(piece.shape[0] for piece in pieces), pieces[0].shape[1]
-    block = tile_width(width, 896)
+    block = tile_width(width, 1792)
     whole = pl.BlockSpec(routes.shape, lambda i: (0, 0))
     parts = 3 if weighted else 1
     return pl.pallas_call(
@@ -225,6 +228,34 @@
             transcendentals=0,
         ),
     )(left, right)
+
+
+def sum_kernel(placed_ref, *refs):
+    out_ref = refs[-1]
+    rows = jnp.concatenate([ref[...] for ref in refs[:-1]])
+    out_ref[...] = lax.dot_general(
+        placed_ref[...], rows, (((0,), (0,)), ((), ())), preferred_element_type=jnp.float32
+    ).astype(jnp.bfloat16)
+
+
+def sum_rows(placed, pieces):
+    row_total, tok_count = placed.shape
+    width = pieces[0].shape[1]
+    block = tile_width(width, 1792)
+    return pl.pallas_call(
+        sum_kernel,
+        grid=(width // block,),
+        in_specs=[pl.BlockSpec(placed.shape, lambda i: (0, 0))]
+        + [pl.BlockSpec((piece.shape[0], block), lambda i: (0, i)) for piece in pieces],
+        out_specs=pl.BlockSpec((tok_count, block), lambda i: (0, i)),
+        out_shape=jax.ShapeDtypeStruct((tok_count, width), jnp.bfloat16),
+        compiler_params=pltpu.CompilerParams(vmem_limit_bytes=VMEM_BYTES),
+        cost_estimate=pl.CostEstimate(
+            flops=2 * row_total * tok_count * width,
+            bytes_accessed=2 * (tok_count + row_total) * width,
+            transcendentals=0,
+        ),
+    )(placed, *pieces)
 
 
 def held_kernel(right_dim, block, groups, left_ref, right_ref, *out_refs):
@@ -293,7 +324,9 @@
 
 
 def send_back(out_pieces, inner):
-    return trade(regroup(trade(out_pieces, inner), inner), 1)
+    moved = trade(out_pieces, inner)
+    runs = [trade(regroup(run, inner), 1) for run in (moved[:1], moved[1:])]
+    return [run[k] for k in range(inner) for run in runs]
 
 
 def dp_swap(part):
@@ -378,7 +411,7 @@
     table = (routes, gates)
 
     mine = own[None]
-    token_pieces = gather_rows(
+    *token_pieces, placed = gather_rows(
         mine, *table, tokens, expert_count, slot_count, False, outer, 1
     )
     moved = trade(token_pieces, inner)
@@ -388,7 +421,7 @@
         run = trade(run, 1)
         expert_rows.append(jnp.concatenate(regroup(run, outer // 2)))
 
-    cot = gather_rows(mine, *table, cotangent, expert_count, slot_count, True, inner, outer)
+    cot = gather_rows(mine, *table, cotangent, expert_count, slot_count, True, inner, outer)[:-1]
     cot = trade(cot, 1)
     cot = regroup(cot, outer)
     scaled_cot = jnp.concatenate(trade(cot, inner))
@@ -411,7 +444,7 @@
         jnp.concatenate(expert_rows), hidden_cot, contract_rows, preferred_element_type=jnp.float32
     ).astype(jnp.bfloat16)
     mixed = combine_rows(mine, *table, back_out, expert_count, True, outer)
-    token_grad = combine_rows(mine, *table, back_grad, expert_count, False, 1)
+    token_grad = sum_rows(placed, back_grad)
     return (mixed, token_grad, hidden_grad[None], output_grad[None])
 
 

time: 224 us -> 230 us (1.027); the launches traced: 222 us -> 226 us
  starting transfers between devices: 60.7 us -> 64.2 us
    ppermute x30 -> x33, starting transfers between devices: 55.1 us -> 58.6 us  [trade(): got[k] = lax.ppermute(pieces[k], 'expert', pairs)]
    pallas_call x2 -> x1, Pallas kernels: 6.67 us -> 3.21 us  [combine_rows(): pl.pallas_call(functools.partial(combine_kernel, weighted, expert_count,...]
    ppermute x30 -> x33, waiting for transfers between devices: 81.8 us -> 80.4 us  [trade(): got[k] = lax.ppermute(pieces[k], 'expert', pairs)]
  transfers between devices with their start and end apart: 36 -> 39, of which waited for: 17 -> 18; matrix products, arithmetic and copies ran while one was open for 10% -> 11% of each run, Pallas kernels for 13% -> 12%
where the time goes in v4:
time: 230 us; the launch traced here: 226 us
  waiting for transfers between devices  98.8 us (43%)
  starting transfers between devices  64.2 us (28%)
  Pallas kernels  33.8 us (15%)
  matrix products  16.2 us (7%)
  local copies, waits for them, and re-layouts  7.22 us (3%)
  other arithmetic  4.14 us (2%)
    ppermute x33, waiting for transfers between devices, trade(): got[k] = lax.ppermute(pieces[k], 'expert', pairs)  80.4 us
    ppermute x33, starting transfers between devices, trade(): got[k] = lax.ppermute(pieces[k], 'expert', pairs)  58.6 us
    ppermute x6, waiting for transfers between devices, dp_swap(): return lax.ppermute(part, 'dp', [(0, 1), (1, 0)])  18.4 us
    dot_general x1, matrix products, body(): lax.dot_general(jnp.concatenate(expert_rows), hidden_cot, contract_rows,...  11.1 us
    pallas_call x3, Pallas kernels, held_product(): pl.pallas_call(functools.partial(held_kernel, right_dim, block, groups),...  10.2 us
    pallas_call x6, Pallas kernels, part_product(): pl.pallas_call(functools.partial(kernel, first), in_specs=[pl.BlockSpec(m...  6.76 us
    pallas_call x2, Pallas kernels, gather_rows(): pl.pallas_call(functools.partial(gather_kernel, scaled, slot_count, outer...  6.34 us
    ppermute x6, starting transfers between devices, dp_swap(): return lax.ppermute(part, 'dp', [(0, 1), (1, 0)])  5.61 us
  transfers between devices with their start and end apart: 39, of which 18 were waited for; matrix products, arithmetic and copies ran while one was open for 11% of the time, Pallas kernels for 12%

profile of v4, /device:TPU:13, one launch (start us, length us, event | category | flops | bytes accessed | tf_op | source)
XLA Modules:
  0.0 225.7 jit_solution(12828327441920383018)
XLA Ops:
  0.6 3.1 %shard_map.93 = (bf16[64,3584]{1,0:T(8,128)(2,1)}, bf16[64,3584]{1,0:T(8,128)(2,1)}, bf16[64,3584]{1,0:T(8,128)(2,1)}, bf16[64,3584]{1,0:T(8,128)(2,1)}, bf16[256,256]{1,0:T(8,128)(2,1)}) custom-call(s32[1]{0:T(128)} %bitcast.own_ref, s32[8,256]{1,0:T(8,128)} %bitcast.12, f32[8,256]{1,0:T(8,128)} %bitcast.15, bf16[256,3584]{1,0:T(8,128)(2,1)} %rows_ref.2), custom_call_target="tpu_custom_call" | custom-call | flops 469762048 | bytes 3670016 | tf_op jit(solution)/shard_map/pallas_call | solution.py:86
  4.0 2.3 %collective-permute-start.6 = (bf16[64,3584]{1,0:T(8,128)(2,1)}, bf16[64,3584]{1,0:T(8,128)(2,1)S(1)}, u32[]{:S(2)}, u32[]{:S(2)}) collective-permute-start(bf16[64,3584]{1,0:T(8,128)(2,1)} %get-tuple-element.37), channel_id=1, source_target_pairs={{0,8},{1,9},{2,10},{3,11},{4,12},{5,13},{6,14},{7,15},{8,0},{9,1},... | collective-permute-start | bytes 1376264 | tf_op jit(solution)/shard_map/ppermute | solution.py:312
  6.4 3.2 %shard_map.102 = (bf16[64,3584]{1,0:T(8,128)(2,1)}, bf16[64,3584]{1,0:T(8,128)(2,1)}, bf16[64,3584]{1,0:T(8,128)(2,1)}, bf16[64,3584]{1,0:T(8,128)(2,1)}, bf16[256,256]{1,0:T(8,128)(2,1)}) custom-call(s32[1]{0:T(128)} %bitcast.own_ref, s32[8,256]{1,0:T(8,128)} %bitcast.13, f32[8,256]{1,0:T(8,128)} %bitcast.16, bf16[256,3584]{1,0:T(8,128)(2,1)} %rows_ref.3), custom_call_target="tpu_custom_call" | custom-call | flops 469762048 | bytes 3670016 | tf_op jit(solution)/shard_map/pallas_call | solution.py:86
  11.5 3.1 %copy-done = bf16[1,1024,3584]{2,1,0:T(8,128)(2,1)S(1)} copy-done((bf16[1,1024,3584]{2,1,0:T(8,128)(2,1)S(1)}, bf16[1,1024,3584]{2,1,0:T(8,128)(2,1)}, u32[]{:S(2)}) %copy-start) | copy-done | bytes 7340056
  14.5 5.3 %shard_map.94 = (bf16[3584,2048]{1,0:T(8,128)(2,1)S(1)}, bf16[1024,3584]{1,0:T(8,128)(2,1)S(1)}) custom-call(bf16[3584,2048]{1,0:T(8,128)(2,1)} %bitcast.18, bf16[1024,3584]{1,0:T(8,128)(2,1)S(1)} %bitcast.11), custom_call_target="tpu_custom_call" | custom-call | bytes 44040192 | tf_op jit(solution)/shard_map/pallas_call | solution.py:197
  21.5 1.9 collective-permute-done.23
  23.4 10.0 %collective-permute-done.24 = bf16[64,3584]{1,0:T(8,128)(2,1)S(1)} collective-permute-done((bf16[64,3584]{1,0:T(8,128)(2,1)S(1)}, bf16[64,3584]{1,0:T(8,128)(2,1)S(1)}, u32[]{:S(2)}, u32[]{:S(2)}) %collective-permute-start.24) | collective-permute-done | bytes 458784 | tf_op jit(solution)/shard_map/ppermute | solution.py:312
  35.0 2.2 collective-permute-start.26
  37.7 8.2 %collective-permute-done.7 = bf16[64,3584]{1,0:T(8,128)(2,1)S(1)} collective-permute-done((bf16[64,3584]{1,0:T(8,128)(2,1)}, bf16[64,3584]{1,0:T(8,128)(2,1)S(1)}, u32[]{:S(2)}, u32[]{:S(2)}) %collective-permute-start.7) | collective-permute-done | bytes 458784 | tf_op jit(solution)/shard_map/ppermute | solution.py:312
  45.9 22.8 %collective-permute-start.1 = (bf16[32,3584]{1,0:T(8,128)(2,1)S(1)}, bf16[32,3584]{1,0:T(8,128)(2,1)S(1)}, u32[]{:S(2)}, u32[]{:S(2)}) collective-permute-start(bf16[32,3584]{1,0:T(8,128)(2,1)S(1)} %pad_maximum_fusion.9), channel_id=1, source_target_pairs={{0,1},{1,0},{2,3},{3,2},{4,5},{5,4},{6,7},{7,6},{8,9},{9,8},{10,11... | collective-permute-start | bytes 688136 | tf_op jit(solution)/shard_map/ppermute | solution.py:312
  70.0 6.5 %collective-permute-done.2 = bf16[32,3584]{1,0:T(8,128)(2,1)S(1)} collective-permute-done((bf16[32,3584]{1,0:T(8,128)(2,1)S(1)}, bf16[32,3584]{1,0:T(8,128)(2,1)S(1)}, u32[]{:S(2)}, u32[]{:S(2)}) %collective-permute-start.2) | collective-permute-done | bytes 229408 | tf_op jit(solution)/shard_map/ppermute | solution.py:312
  78.0 6.3 %collective-permute-done.3 = bf16[32,3584]{1,0:T(8,128)(2,1)S(1)} collective-permute-done((bf16[32,3584]{1,0:T(8,128)(2,1)S(1)}, bf16[32,3584]{1,0:T(8,128)(2,1)S(1)}, u32[]{:S(2)}, u32[]{:S(2)}) %collective-permute-start.3) | collective-permute-done | bytes 229408 | tf_op jit(solution)/shard_map/ppermute | solution.py:312
  96.2 4.2 %collective-permute-done.10 = bf16[32,3584]{1,0:T(8,128)(2,1)S(1)} collective-permute-done((bf16[32,3584]{1,0:T(8,128)(2,1)S(1)}, bf16[32,3584]{1,0:T(8,128)(2,1)S(1)}, u32[]{:S(2)}, u32[]{:S(2)}) %collective-permute-start.10) | collective-permute-done | bytes 229408 | tf_op jit(solution)/shard_map/ppermute | solution.py:312
  104.6 2.3 %shard_map.97 = (bf16[64,3584]{1,0:T(8,128)(2,1)S(1)}, bf16[64,3584]{1,0:T(8,128)(2,1)S(1)}) custom-call(bf16[128,1024]{1,0:T(8,128)(2,1)S(1)} %multiply_convert_fusion.2.left_ref, bf16[1024,3584]{1,0:T(8,128)(2,1)S(1)} %get-tuple-element.35.right_ref), custom_call_target="tpu_custom_call" | custom-call | flops 939524096 | bytes 8519680 | tf_op jit(solution)/shard_map/pallas_call | solution.py:279
  107.0 12.8 %collective-permute-done.11 = bf16[128,1024]{1,0:T(8,128)(2,1)S(1)} collective-permute-done((bf16[128,1024]{1,0:T(8,128)(2,1)S(1)}, bf16[128,1024]{1,0:T(8,128)(2,1)S(1)}, u32[]{:S(2)}, u32[]{:S(2)}) %collective-permute-start.11) | collective-permute-done | bytes 262176 | tf_op jit(solution)/shard_map/ppermute | solution.py:333
  119.8 5.6 %collective-permute-done.12 = bf16[128,1024]{1,0:T(8,128)(2,1)S(1)} collective-permute-done((bf16[128,1024]{1,0:T(8,128)(2,1)S(1)}, bf16[128,1024]{1,0:T(8,128)(2,1)S(1)}, u32[]{:S(2)}, u32[]{:S(2)}) %collective-permute-start.12) | collective-permute-done | bytes 262176 | tf_op jit(solution)/shard_map/ppermute | solution.py:333
  125.6 2.3 %shard_map.100 = (bf16[64,3584]{1,0:T(8,128)(2,1)S(1)}, bf16[64,3584]{1,0:T(8,128)(2,1)S(1)}) custom-call(bf16[128,1024]{1,0:T(8,128)(2,1)S(1)} %multiply_convert_fusion.1.left_ref, bf16[1024,3584]{1,0:T(8,128)(2,1)S(1)} %get-tuple-element.35.right_ref), custom_call_target="tpu_custom_call" | custom-call | flops 939524096 | bytes 8519680 | tf_op jit(solution)/shard_map/pallas_call | solution.py:279
  134.5 5.6 %shard_map.105 = (bf16[64,3584]{1,0:T(8,128)(2,1)S(1)}, bf16[64,3584]{1,0:T(8,128)(2,1)S(1)}, bf16[64,3584]{1,0:T(8,128)(2,1)S(1)}, bf16[64,3584]{1,0:T(8,128)(2,1)S(1)}) custom-call(bf16[256,2048]{1,0:T(8,128)(2,1)S(1)} %pad_maximum_fusion.1.left_ref, bf16[3584,2048]{1,0:T(8,128)(2,1)S(1)} %get-tuple-element.34.right_ref), custom_call_target="tpu_custom_call" | custom-call | flops 3758096384 | bytes 17563648 | tf_op jit(solution)/shard_map/pallas_call | solution.py:279
  140.2 11.1 %fusion = bf16[1,3584,2048]{2,1,0:T(8,128)(2,1)} fusion(bf16[256,3584]{1,0:T(8,128)(2,1)} %copy-done.4, bf16[256,1024]{1,0:T(8,128)(2,1)} %get-tuple-element.61, bf16[256,1024]{1,0:T(8,128)(2,1)S(1)} %get-tuple-element.60), kind=kOutput, calls=%fused_computation.1 | convolution fusion | flops 3767533568 | bytes 17563648 | tf_op jit(solution)/shard_map/dot_general | solution.py:443
  151.3 5.2 %fusion.1 = bf16[1,1024,3584]{2,1,0:T(8,128)(2,1)} fusion(bf16[256,3584]{1,0:T(8,128)(2,1)S(1)} %constant_dynamic-update-slice_fusion.left_ref, bf16[128,1024]{1,0:T(8,128)(2,1)S(1)} %multiply_convert_fusion.1.left_ref, bf16[128,1024]{1,0:T(8,128)(2,1)S(1)} %multiply_convert_fusion.2.left_ref), kind=kOutput, calls=%fused_computation.3 | convolution fusion | flops 1883766784 | bytes 9699328 | tf_op jit(solution)/shard_map/dot_general | solution.py:440
  159.9 3.0 %collective-permute-start.33 = (bf16[32,3584]{1,0:T(8,128)(2,1)S(1)}, bf16[32,3584]{1,0:T(8,128)(2,1)S(1)}, u32[]{:S(2)}, u32[]{:S(2)}) collective-permute-start(bf16[32,3584]{1,0:T(8,128)(2,1)S(1)} %pad_maximum_fusion.17), channel_id=1, source_target_pairs={{0,4},{1,5},{2,6},{3,7},{4,0},{5,1},{6,2},{7,3},{8,12},{9,13},{10,... | collective-permute-start | bytes 688136 | tf_op jit(solution)/shard_map/ppermute | solution.py:312
  164.0 4.1 %collective-permute-done.31 = bf16[64,3584]{1,0:T(8,128)(2,1)S(1)} collective-permute-done((bf16[64,3584]{1,0:T(8,128)(2,1)S(1)}, bf16[64,3584]{1,0:T(8,128)(2,1)S(1)}, u32[]{:S(2)}, u32[]{:S(2)}) %collective-permute-start.31) | collective-permute-done | bytes 458784 | tf_op jit(solution)/shard_map/ppermute | solution.py:312
  168.1 3.5 %collective-permute-start.35 = (bf16[32,3584]{1,0:T(8,128)(2,1)S(1)}, bf16[32,3584]{1,0:T(8,128)(2,1)S(1)}, u32[]{:S(2)}, u32[]{:S(2)}) collective-permute-start(bf16[32,3584]{1,0:T(8,128)(2,1)S(1)} %pad_maximum_fusion.19), channel_id=1, source_target_pairs={{0,8},{1,9},{2,10},{3,11},{4,12},{5,13},{6,14},{7,15},{8,0},{9,1},... | collective-permute-start | bytes 688136 | tf_op jit(solution)/shard_map/ppermute | solution.py:312
  171.7 6.9 %collective-permute-done.32 = bf16[64,3584]{1,0:T(8,128)(2,1)S(1)} collective-permute-done((bf16[64,3584]{1,0:T(8,128)(2,1)S(1)}, bf16[64,3584]{1,0:T(8,128)(2,1)S(1)}, u32[]{:S(2)}, u32[]{:S(2)}) %collective-permute-start.32) | collective-permute-done | bytes 458784 | tf_op jit(solution)/shard_map/ppermute | solution.py:312
  178.8 4.8 %collective-permute-start.34 = (bf16[32,3584]{1,0:T(8,128)(2,1)S(1)}, bf16[32,3584]{1,0:T(8,128)(2,1)S(1)}, u32[]{:S(2)}, u32[]{:S(2)}) collective-permute-start(bf16[32,3584]{1,0:T(8,128)(2,1)S(1)} %pad_maximum_fusion.18), channel_id=1, source_target_pairs={{0,4},{1,5},{2,6},{3,7},{4,0},{5,1},{6,2},{7,3},{8,12},{9,13},{10,... | collective-permute-start | bytes 688136 | tf_op jit(solution)/shard_map/ppermute | solution.py:312
  186.8 5.6 %collective-permute-done.37.refs_6_ = bf16[32,3584]{1,0:T(8,128)(2,1)S(1)} collective-permute-done((bf16[32,3584]{1,0:T(8,128)(2,1)S(1)}, bf16[32,3584]{1,0:T(8,128)(2,1)S(1)}, u32[]{:S(2)}, u32[]{:S(2)}) %collective-permute-start.37) | collective-permute-done | bytes 229408 | tf_op jit(solution)/shard_map/ppermute | solution.py:312
  193.0 2.4 %collective-permute-done.34.refs_3_ = bf16[32,3584]{1,0:T(8,128)(2,1)S(1)} collective-permute-done((bf16[32,3584]{1,0:T(8,128)(2,1)S(1)}, bf16[32,3584]{1,0:T(8,128)(2,1)S(1)}, u32[]{:S(2)}, u32[]{:S(2)}) %collective-permute-start.34) | collective-permute-done | bytes 229408 | tf_op jit(solution)/shard_map/ppermute | solution.py:312
  195.9 9.3 %collective-permute-done.36.refs_5_ = bf16[32,3584]{1,0:T(8,128)(2,1)S(1)} collective-permute-done((bf16[32,3584]{1,0:T(8,128)(2,1)S(1)}, bf16[32,3584]{1,0:T(8,128)(2,1)S(1)}, u32[]{:S(2)}, u32[]{:S(2)}) %collective-permute-start.36) | collective-permute-done | bytes 229408 | tf_op jit(solution)/shard_map/ppermute | solution.py:312
  205.8 6.4 %collective-permute-done.38.refs_7_ = bf16[32,3584]{1,0:T(8,128)(2,1)S(1)} collective-permute-done((bf16[32,3584]{1,0:T(8,128)(2,1)S(1)}, bf16[32,3584]{1,0:T(8,128)(2,1)S(1)}, u32[]{:S(2)}, u32[]{:S(2)}) %collective-permute-start.38) | collective-permute-done | bytes 229408 | tf_op jit(solution)/shard_map/ppermute | solution.py:312
  213.1 2.0 shard_map.106
  215.2 7.3 %collective-permute-done.21.refs_7_ = bf16[48,3584]{1,0:T(8,128)(2,1)S(1)} collective-permute-done((bf16[48,3584]{1,0:T(8,128)(2,1)S(1)}, bf16[48,3584]{1,0:T(8,128)(2,1)S(1)}, u32[]{:S(2)}, u32[]{:S(2)}) %collective-permute-start.21) | collective-permute-done | bytes 344096 | tf_op jit(solution)/shard_map/ppermute | solution.py:312
  222.5 3.2 %shard_map.101 = bf16[256,3584]{1,0:T(8,128)(2,1)} custom-call(s32[1]{0:T(128)} %bitcast.own_ref, s32[8,256]{1,0:T(8,128)S(1)} %bitcast.14, f32[8,256]{1,0:T(8,128)S(1)} %bitcast.17, bf16[16,3584]{1,0:T(8,128)(2,1)S(1)} %get-tuple-element.123.refs_0_, bf16[48,3584]{1,0:T(8,128)(2,1)S(1)} %pad_maximum_fusion.5.refs_1_, ...), custom_call_target="tpu_custom_call" | custom-call | flops 1409286144 | bytes 3670016 | tf_op jit(solution)/shard_map/pallas_call | solution.py:153
  (141 shorter events, 41.9 us)
Async XLA Ops:
  3.7 33.5 %collective-permute-start = (bf16[64,3584]{1,0:T(8,128)(2,1)}, bf16[64,3584]{1,0:T(8,128)(2,1)S(1)}, u32[]{:S(2)}, u32[]{:S(2)}) collective-permute-start(bf16[64,3584]{1,0:T(8,128)(2,1)} %get-tuple-element.33), channel_id=1, source_target_pairs={{0,4},{1,5},{2,6},{3,7},{4,0},{5,1},{6,2},{7,3},{8,12},{9,13},{10,... | collective-permute-start | bytes 1376264 | tf_op jit(solution)/shard_map/ppermute | solution.py:312
  4.0 82.7 %collective-permute-start.6 = (bf16[64,3584]{1,0:T(8,128)(2,1)}, bf16[64,3584]{1,0:T(8,128)(2,1)S(1)}, u32[]{:S(2)}, u32[]{:S(2)}) collective-permute-start(bf16[64,3584]{1,0:T(8,128)(2,1)} %get-tuple-element.37), channel_id=1, source_target_pairs={{0,8},{1,9},{2,10},{3,11},{4,12},{5,13},{6,14},{7,15},{8,0},{9,1},... | collective-permute-start | bytes 1376264 | tf_op jit(solution)/shard_map/ppermute | solution.py:312
  6.3 39.6 %collective-permute-start.7 = (bf16[64,3584]{1,0:T(8,128)(2,1)}, bf16[64,3584]{1,0:T(8,128)(2,1)S(1)}, u32[]{:S(2)}, u32[]{:S(2)}) collective-permute-start(bf16[64,3584]{1,0:T(8,128)(2,1)} %get-tuple-element.38), channel_id=1, source_target_pairs={{0,12},{1,13},{2,14},{3,15},{4,8},{5,9},{6,10},{7,11},{8,4},{9,5},... | collective-permute-start | bytes 1376264 | tf_op jit(solution)/shard_map/ppermute | solution.py:312
  11.2 12.2 %collective-permute-start.23 = (bf16[64,3584]{1,0:T(8,128)(2,1)}, bf16[64,3584]{1,0:T(8,128)(2,1)S(1)}, u32[]{:S(2)}, u32[]{:S(2)}) collective-permute-start(bf16[64,3584]{1,0:T(8,128)(2,1)} %get-tuple-element.46), channel_id=1, source_target_pairs={{0,2},{1,3},{2,0},{3,1},{4,6},{5,7},{6,4},{7,5},{8,10},{9,11},{10,... | collective-permute-start | bytes 1376264 | tf_op jit(solution)/shard_map/ppermute | solution.py:312
  19.9 13.6 %collective-permute-start.24 = (bf16[64,3584]{1,0:T(8,128)(2,1)S(1)}, bf16[64,3584]{1,0:T(8,128)(2,1)S(1)}, u32[]{:S(2)}, u32[]{:S(2)}) collective-permute-start(bf16[64,3584]{1,0:T(8,128)(2,1)S(1)} %copy-done.7), channel_id=1, source_target_pairs={{0,3},{1,2},{2,1},{3,0},{4,7},{5,6},{6,5},{7,4},{8,11},{9,10},{10,... | collective-permute-start | bytes 1376264 | tf_op jit(solution)/shard_map/ppermute | solution.py:312
  33.5 55.0 %collective-permute-start.25 = (bf16[64,3584]{1,0:T(8,128)(2,1)S(1)}, bf16[64,3584]{1,0:T(8,128)(2,1)S(1)}, u32[]{:S(2)}, u32[]{:S(2)}) collective-permute-start(bf16[64,3584]{1,0:T(8,128)(2,1)S(1)} %pad_maximum_fusion.2), channel_id=1, source_target_pairs={{0,4},{1,5},{2,6},{3,7},{4,0},{5,1},{6,2},{7,3},{8,12},{9,13},{10,... | collective-permute-start | bytes 1376264 | tf_op jit(solution)/shard_map/ppermute | solution.py:312
  35.0 54.6 %collective-permute-start.26 = (bf16[64,3584]{1,0:T(8,128)(2,1)S(1)}, bf16[64,3584]{1,0:T(8,128)(2,1)S(1)}, u32[]{:S(2)}, u32[]{:S(2)}) collective-permute-start(bf16[64,3584]{1,0:T(8,128)(2,1)S(1)} %pad_maximum_fusion.3), channel_id=1, source_target_pairs={{0,8},{1,9},{2,10},{3,11},{4,12},{5,13},{6,14},{7,15},{8,0},{9,1},... | collective-permute-start | bytes 1376264 | tf_op jit(solution)/shard_map/ppermute | solution.py:312
  37.3 53.6 %collective-permute-start.27 = (bf16[64,3584]{1,0:T(8,128)(2,1)S(1)}, bf16[64,3584]{1,0:T(8,128)(2,1)S(1)}, u32[]{:S(2)}, u32[]{:S(2)}) collective-permute-start(bf16[64,3584]{1,0:T(8,128)(2,1)S(1)} %pad_maximum_fusion.4), channel_id=1, source_target_pairs={{0,12},{1,13},{2,14},{3,15},{4,8},{5,9},{6,10},{7,11},{8,4},{9,5},... | collective-permute-start | bytes 1376264 | tf_op jit(solution)/shard_map/ppermute | solution.py:312
  45.9 23.9 %collective-permute-start.1 = (bf16[32,3584]{1,0:T(8,128)(2,1)S(1)}, bf16[32,3584]{1,0:T(8,128)(2,1)S(1)}, u32[]{:S(2)}, u32[]{:S(2)}) collective-permute-start(bf16[32,3584]{1,0:T(8,128)(2,1)S(1)} %pad_maximum_fusion.9), channel_id=1, source_target_pairs={{0,1},{1,0},{2,3},{3,2},{4,5},{5,4},{6,7},{7,6},{8,9},{9,8},{10,11... | collective-permute-start | bytes 688136 | tf_op jit(solution)/shard_map/ppermute | solution.py:312
  88.5 11.8 %collective-permute-start.10 = (bf16[32,3584]{1,0:T(8,128)(2,1)S(1)}, bf16[32,3584]{1,0:T(8,128)(2,1)S(1)}, u32[]{:S(2)}, u32[]{:S(2)}) collective-permute-start(bf16[32,3584]{1,0:T(8,128)(2,1)S(1)} %pad_maximum_fusion.14), channel_id=1, source_target_pairs={{0,3},{1,2},{2,1},{3,0},{4,7},{5,6},{6,5},{7,4},{8,11},{9,10},{10,... | collective-permute-start | bytes 688136 | tf_op jit(solution)/shard_map/ppermute | solution.py:312
  89.6 14.4 %collective-permute-start.4 = (bf16[128,1024]{1,0:T(8,128)(2,1)S(1)}, bf16[128,1024]{1,0:T(8,128)(2,1)S(1)}, u32[]{:S(2)}, u32[]{:S(2)}) collective-permute-start(bf16[128,1024]{1,0:T(8,128)(2,1)S(1)} %shard_map.95), channel_id=1, source_target_pairs={{0,16},{16,0},{1,17},{17,1},{2,18},{18,2},{3,19},{19,3},{4,20},{20... | collective-permute-start | bytes 786440 | tf_op jit(solution)/shard_map/ppermute | solution.py:333
  90.9 13.5 %collective-permute-start.5 = (bf16[128,1024]{1,0:T(8,128)(2,1)S(1)}, bf16[128,1024]{1,0:T(8,128)(2,1)S(1)}, u32[]{:S(2)}, u32[]{:S(2)}) collective-permute-start(bf16[128,1024]{1,0:T(8,128)(2,1)S(1)} %shard_map.96), channel_id=1, source_target_pairs={{0,16},{16,0},{1,17},{17,1},{2,18},{18,2},{3,19},{19,3},{4,20},{20... | collective-permute-start | bytes 786440 | tf_op jit(solution)/shard_map/ppermute | solution.py:333
  92.4 38.0 %collective-permute-start.28 = (bf16[256,512]{1,0:T(8,128)(2,1)S(1)}, bf16[256,512]{1,0:T(8,128)(2,1)S(1)}, u32[]{:S(2)}, u32[]{:S(2)}) collective-permute-start(bf16[256,512]{1,0:T(8,128)(2,1)S(1)} %shard_map.103), channel_id=1, source_target_pairs={{0,16},{16,0},{1,17},{17,1},{2,18},{18,2},{3,19},{19,3},{4,20},{20... | collective-permute-start | bytes 786440 | tf_op jit(solution)/shard_map/ppermute | solution.py:333
  94.9 36.9 %collective-permute-start.29 = (bf16[256,512]{1,0:T(8,128)(2,1)S(1)}, bf16[256,512]{1,0:T(8,128)(2,1)S(1)}, u32[]{:S(2)}, u32[]{:S(2)}) collective-permute-start(bf16[256,512]{1,0:T(8,128)(2,1)S(1)} %shard_map.104), channel_id=1, source_target_pairs={{0,16},{16,0},{1,17},{17,1},{2,18},{18,2},{3,19},{19,3},{4,20},{20... | collective-permute-start | bytes 786440 | tf_op jit(solution)/shard_map/ppermute | solution.py:333
  101.7 18.1 %collective-permute-start.11 = (bf16[128,1024]{1,0:T(8,128)(2,1)S(1)}, bf16[128,1024]{1,0:T(8,128)(2,1)S(1)}, u32[]{:S(2)}, u32[]{:S(2)}) collective-permute-start(bf16[128,1024]{1,0:T(8,128)(2,1)S(1)} %shard_map.98), channel_id=1, source_target_pairs={{0,16},{16,0},{1,17},{17,1},{2,18},{18,2},{3,19},{19,3},{4,20},{20... | collective-permute-start | bytes 786440 | tf_op jit(solution)/shard_map/ppermute | solution.py:333
  104.0 21.4 %collective-permute-start.12 = (bf16[128,1024]{1,0:T(8,128)(2,1)S(1)}, bf16[128,1024]{1,0:T(8,128)(2,1)S(1)}, u32[]{:S(2)}, u32[]{:S(2)}) collective-permute-start(bf16[128,1024]{1,0:T(8,128)(2,1)S(1)} %shard_map.99), channel_id=1, source_target_pairs={{0,16},{16,0},{1,17},{17,1},{2,18},{18,2},{3,19},{19,3},{4,20},{20... | collective-permute-start | bytes 786440 | tf_op jit(solution)/shard_map/ppermute | solution.py:333
  107.0 49.5 %collective-permute-start.13 = (bf16[64,3584]{1,0:T(8,128)(2,1)S(1)}, bf16[64,3584]{1,0:T(8,128)(2,1)}, u32[]{:S(2)}, u32[]{:S(2)}) collective-permute-start(bf16[64,3584]{1,0:T(8,128)(2,1)S(1)} %get-tuple-element.40), channel_id=1, source_target_pairs={{0,4},{1,5},{2,6},{3,7},{4,0},{5,1},{6,2},{7,3},{8,12},{9,13},{10,... | collective-permute-start | bytes 1376264 | tf_op jit(solution)/shard_map/ppermute | solution.py:312
  128.0 56.8 %collective-permute-start.20 = (bf16[16,3584]{1,0:T(8,128)(2,1)S(1)}, bf16[16,3584]{1,0:T(8,128)(2,1)S(1)}, u32[]{:S(2)}, u32[]{:S(2)}) collective-permute-start(bf16[16,3584]{1,0:T(8,128)(2,1)S(1)} %get-tuple-element.120), channel_id=1, source_target_pairs={{0,3},{1,2},{2,1},{3,0},{4,7},{5,6},{6,5},{7,4},{8,11},{9,10},{10,... | collective-permute-start | bytes 344072 | tf_op jit(solution)/shard_map/ppermute | solution.py:312
  129.9 30.0 %collective-permute-start.14 = (bf16[64,3584]{1,0:T(8,128)(2,1)S(1)}, bf16[64,3584]{1,0:T(8,128)(2,1)}, u32[]{:S(2)}, u32[]{:S(2)}) collective-permute-start(bf16[64,3584]{1,0:T(8,128)(2,1)S(1)} %get-tuple-element.41), channel_id=1, source_target_pairs={{0,8},{1,9},{2,10},{3,11},{4,12},{5,13},{6,14},{7,15},{8,0},{9,1},... | collective-permute-start | bytes 1376264 | tf_op jit(solution)/shard_map/ppermute | solution.py:312
  130.4 48.4 %collective-permute-start.15 = (bf16[64,3584]{1,0:T(8,128)(2,1)S(1)}, bf16[64,3584]{1,0:T(8,128)(2,1)}, u32[]{:S(2)}, u32[]{:S(2)}) collective-permute-start(bf16[64,3584]{1,0:T(8,128)(2,1)S(1)} %get-tuple-element.42), channel_id=1, source_target_pairs={{0,12},{1,13},{2,14},{3,15},{4,8},{5,9},{6,10},{7,11},{8,4},{9,5},... | collective-permute-start | bytes 1376264 | tf_op jit(solution)/shard_map/ppermute | solution.py:312
  140.1 18.0 %collective-permute-start.30 = (bf16[64,3584]{1,0:T(8,128)(2,1)S(1)}, bf16[64,3584]{1,0:T(8,128)(2,1)S(1)}, u32[]{:S(2)}, u32[]{:S(2)}) collective-permute-start(bf16[64,3584]{1,0:T(8,128)(2,1)S(1)} %get-tuple-element.57), channel_id=1, source_target_pairs={{0,1},{1,0},{2,3},{3,2},{4,5},{5,4},{6,7},{7,6},{8,9},{9,8},{10,11... | collective-permute-start | bytes 1376264 | tf_op jit(solution)/shard_map/ppermute | solution.py:312
  156.5 11.7 %collective-permute-start.31 = (bf16[64,3584]{1,0:T(8,128)(2,1)S(1)}, bf16[64,3584]{1,0:T(8,128)(2,1)S(1)}, u32[]{:S(2)}, u32[]{:S(2)}) collective-permute-start(bf16[64,3584]{1,0:T(8,128)(2,1)S(1)} %get-tuple-element.58), channel_id=1, source_target_pairs={{0,2},{1,3},{2,0},{3,1},{4,6},{5,7},{6,4},{7,5},{8,10},{9,11},{10,... | collective-permute-start | bytes 1376264 | tf_op jit(solution)/shard_map/ppermute | solution.py:312
  158.2 20.4 %collective-permute-start.32 = (bf16[64,3584]{1,0:T(8,128)(2,1)S(1)}, bf16[64,3584]{1,0:T(8,128)(2,1)S(1)}, u32[]{:S(2)}, u32[]{:S(2)}) collective-permute-start(bf16[64,3584]{1,0:T(8,128)(2,1)S(1)} %get-tuple-element.59), channel_id=1, source_target_pairs={{0,3},{1,2},{2,1},{3,0},{4,7},{5,6},{6,5},{7,4},{8,11},{9,10},{10,... | collective-permute-start | bytes 1376264 | tf_op jit(solution)/shard_map/ppermute | solution.py:312
  159.9 25.0 %collective-permute-start.33 = (bf16[32,3584]{1,0:T(8,128)(2,1)S(1)}, bf16[32,3584]{1,0:T(8,128)(2,1)S(1)}, u32[]{:S(2)}, u32[]{:S(2)}) collective-permute-start(bf16[32,3584]{1,0:T(8,128)(2,1)S(1)} %pad_maximum_fusion.17), channel_id=1, source_target_pairs={{0,4},{1,5},{2,6},{3,7},{4,0},{5,1},{6,2},{7,3},{8,12},{9,13},{10,... | collective-permute-start | bytes 688136 | tf_op jit(solution)/shard_map/ppermute | solution.py:312
  168.1 18.0 %collective-permute-start.35 = (bf16[32,3584]{1,0:T(8,128)(2,1)S(1)}, bf16[32,3584]{1,0:T(8,128)(2,1)S(1)}, u32[]{:S(2)}, u32[]{:S(2)}) collective-permute-start(bf16[32,3584]{1,0:T(8,128)(2,1)S(1)} %pad_maximum_fusion.19), channel_id=1, source_target_pairs={{0,8},{1,9},{2,10},{3,11},{4,12},{5,13},{6,14},{7,15},{8,0},{9,1},... | collective-permute-start | bytes 688136 | tf_op jit(solution)/shard_map/ppermute | solution.py:312
  178.5 13.9 %collective-permute-start.37 = (bf16[32,3584]{1,0:T(8,128)(2,1)S(1)}, bf16[32,3584]{1,0:T(8,128)(2,1)S(1)}, u32[]{:S(2)}, u32[]{:S(2)}) collective-permute-start(bf16[32,3584]{1,0:T(8,128)(2,1)S(1)} %pad_maximum_fusion.21), channel_id=1, source_target_pairs={{0,12},{1,13},{2,14},{3,15},{4,8},{5,9},{6,10},{7,11},{8,4},{9,5},... | collective-permute-start | bytes 688136 | tf_op jit(solution)/shard_map/ppermute | solution.py:312
  178.8 16.6 %collective-permute-start.34 = (bf16[32,3584]{1,0:T(8,128)(2,1)S(1)}, bf16[32,3584]{1,0:T(8,128)(2,1)S(1)}, u32[]{:S(2)}, u32[]{:S(2)}) collective-permute-start(bf16[32,3584]{1,0:T(8,128)(2,1)S(1)} %pad_maximum_fusion.18), channel_id=1, source_target_pairs={{0,4},{1,5},{2,6},{3,7},{4,0},{5,1},{6,2},{7,3},{8,12},{9,13},{10,... | collective-permute-start | bytes 688136 | tf_op jit(solution)/shard_map/ppermute | solution.py:312
  184.9 20.3 %collective-permute-start.36 = (bf16[32,3584]{1,0:T(8,128)(2,1)S(1)}, bf16[32,3584]{1,0:T(8,128)(2,1)S(1)}, u32[]{:S(2)}, u32[]{:S(2)}) collective-permute-start(bf16[32,3584]{1,0:T(8,128)(2,1)S(1)} %pad_maximum_fusion.20), channel_id=1, source_target_pairs={{0,8},{1,9},{2,10},{3,11},{4,12},{5,13},{6,14},{7,15},{8,0},{9,1},... | collective-permute-start | bytes 688136 | tf_op jit(solution)/shard_map/ppermute | solution.py:312
  185.0 27.2 %collective-permute-start.38 = (bf16[32,3584]{1,0:T(8,128)(2,1)S(1)}, bf16[32,3584]{1,0:T(8,128)(2,1)S(1)}, u32[]{:S(2)}, u32[]{:S(2)}) collective-permute-start(bf16[32,3584]{1,0:T(8,128)(2,1)S(1)} %pad_maximum_fusion.22), channel_id=1, source_target_pairs={{0,12},{1,13},{2,14},{3,15},{4,8},{5,9},{6,10},{7,11},{8,4},{9,5},... | collective-permute-start | bytes 688136 | tf_op jit(solution)/shard_map/ppermute | solution.py:312
  186.2 29.0 %collective-permute-start.18 = (bf16[16,3584]{1,0:T(8,128)(2,1)S(1)}, bf16[16,3584]{1,0:T(8,128)(2,1)S(1)}, u32[]{:S(2)}, u32[]{:S(2)}) collective-permute-start(bf16[16,3584]{1,0:T(8,128)(2,1)S(1)} %get-tuple-element.121), channel_id=1, source_target_pairs={{0,2},{1,3},{2,0},{3,1},{4,6},{5,7},{6,4},{7,5},{8,10},{9,11},{10,... | collective-permute-start | bytes 344072 | tf_op jit(solution)/shard_map/ppermute | solution.py:312
  192.4 22.7 %collective-permute-start.16 = (bf16[16,3584]{1,0:T(8,128)(2,1)S(1)}, bf16[16,3584]{1,0:T(8,128)(2,1)S(1)}, u32[]{:S(2)}, u32[]{:S(2)}) collective-permute-start(bf16[16,3584]{1,0:T(8,128)(2,1)S(1)} %get-tuple-element.122), channel_id=1, source_target_pairs={{0,1},{1,0},{2,3},{3,2},{4,5},{5,4},{6,7},{7,6},{8,9},{9,8},{10,11... | collective-permute-start | bytes 344072 | tf_op jit(solution)/shard_map/ppermute | solution.py:312
  195.5 19.7 %collective-permute-start.17 = (bf16[48,3584]{1,0:T(8,128)(2,1)S(1)}, bf16[48,3584]{1,0:T(8,128)(2,1)S(1)}, u32[]{:S(2)}, u32[]{:S(2)}) collective-permute-start(bf16[48,3584]{1,0:T(8,128)(2,1)S(1)} %pad_maximum_fusion.6), channel_id=1, source_target_pairs={{0,1},{1,0},{2,3},{3,2},{4,5},{5,4},{6,7},{7,6},{8,9},{9,8},{10,11... | collective-permute-start | bytes 1032200 | tf_op jit(solution)/shard_map/ppermute | solution.py:312
  (15 other events, 127.7 us)
